TPU v7x, 32 devices: a whole 2x2x4 slice. The times are simulated.
32 devices in a mesh: groups: 2 (over x), ctx: 16 (over z, y, core).
Axes of the slice: x: 2, y: 2, z: 4, core: 2. Of those that a mesh axis runs over, the one named last changes fastest.
Arguments:
- tokens: bfloat16 [32, 8192], P('groups', 'ctx'), parts along dimension 0, may hold values from -6 to 6
- attn_gain: float32 [8192], replicated, may hold values from 0.1 to 1.9
- mlp_gain: float32 [8192], replicated, may hold values from 0.1 to 1.9
- q_weight: bfloat16 [8192, 8192], P(None, 'ctx'), may hold values from -0.0625 to 0.0625
- k_weight: bfloat16 [8192, 1024], P('ctx'), may hold values from -0.5 to 0.5
- v_weight: bfloat16 [8192, 1024], P('ctx'), may hold values from -0.0625 to 0.0625
- o_weight: bfloat16 [8192, 8192], P(None, 'ctx'), may hold values from -0.0625 to 0.0625
- gate_weight: bfloat16 [8192, 16384], P(None, 'ctx'), may hold values from -0.0625 to 0.0625
- up_weight: bfloat16 [8192, 16384], P(None, 'ctx'), may hold values from -0.0625 to 0.0625
- down_weight: bfloat16 [16384, 8192], P('ctx'), may hold values from -0.046875 to 0.046875
- prefix_keys: bfloat16 [8192, 1024], P(('groups', 'ctx')), parts along dimension 0, may hold values from -400 to 400
- prefix_values: bfloat16 [8192, 1024], P(('groups', 'ctx')), parts along dimension 0, may hold values from -36 to 36
- suffix_keys: bfloat16 [256, 16, 1024], P(('groups', 'ctx')), parts along dimension 0, may hold values from -18 to 18
- suffix_values: bfloat16 [256, 16, 1024], P(('groups', 'ctx')), parts along dimension 0, may hold values from -18 to 18
- suffix_lengths: int32 [32], P('groups'), parts along dimension 0, may hold values from 1 to 128, as said below
- suffix_table: int32 [32, 8], P(('groups', 'ctx')), parts along dimension 0, may hold values from 0 to 7, as said below
Outputs:
- layer_out: bfloat16 [32, 8192], P('groups', 'ctx'), parts along dimension 0
There are 2 independent parts, one for each index of `groups`. A program takes and returns all parts, laid end to end along the dimension named above; an argument that names none is the same for every part. Nothing has to cross between parts.
Inputs may be any that keep to these rules, and one draw needn't show every extreme that they name: `suffix_lengths`: at most 128; some sample has exactly 128. `suffix_table`: in every aligned block of 1 row, the entries name each of 0 to 7 exactly once.
All inputs are finite; a program needn't handle non-finite values.
Results may differ from a plain program's by a relative error of at most 0.014.
The roundings to bfloat16 on the way count: a program that leaves them out, or rounds other values in their place, can miss the bound.
Values may be sent and summed in bfloat16 or wider, within the bound.
No kernel may reach another device: no remote copies, remote signals or barrier semaphores. Data moves between devices by JAX's collectives and lax.ppermute only.
A program may use at most 128 MiB of HBM per device.

v0:
```python
import math

import jax
import jax.numpy as jnp
from jax import lax
from jax.sharding import PartitionSpec as P

HEADS = 64
KV_HEADS = 8
HEAD_DIM = 128


EPSILON = 1e-05
ROPE_BASE = 500000.0


def rotate(matrix, position, columns):
    pair_index = (columns % HEAD_DIM // 2).astype(jnp.float32)
    frequency = jnp.exp(pair_index * (-2.0 * math.log(ROPE_BASE) / HEAD_DIM))
    angles = position.astype(jnp.float32)[:, None] * frequency[None, :]
    cosine = jnp.cos(angles[:, 0::2])
    sine_part = jnp.sin(angles[:, 0::2])
    even_part = matrix[:, 0::2]
    odd_part = matrix[:, 1::2]
    rotated_even = even_part * cosine - odd_part * sine_part
    rotated_odd = even_part * sine_part + odd_part * cosine
    return jnp.stack([rotated_even, rotated_odd], axis=-1).reshape(matrix.shape)


def normalized_rows(shard_rows, gain_vector):
    self_index = lax.axis_index("ctx")
    feature_width = shard_rows.shape[1]
    gathered_raw = lax.all_gather(shard_rows, "ctx", axis=1, tiled=True)
    widened = gathered_raw.astype(jnp.float32)
    mean_square = jnp.mean(widened * widened, axis=1, keepdims=True)
    gathered = (widened * lax.rsqrt(mean_square + EPSILON) * gain_vector).astype(jnp.bfloat16)
    local_part = lax.dynamic_slice_in_dim(gathered, self_index * feature_width, feature_width, 1)
    return (gathered, local_part)


def body(
    tokens,
    attn_gain,
    mlp_gain,
    q_weight,
    k_weight,
    v_weight,
    o_weight,
    gate_weight,
    up_weight,
    down_weight,
    prefix_keys,
    prefix_values,
    suffix_keys,
    suffix_values,
    suffix_lengths,
    suffix_table,
):
    self_index = lax.axis_index("ctx")
    devices = lax.axis_size("ctx")
    samples = tokens.shape[0]
    own_rows = suffix_table.shape[0]
    group_size = HEADS // KV_HEADS
    score_scale = 1.0 / math.sqrt(HEAD_DIM)
    prefix_rows = prefix_keys.shape[0]
    row_start = self_index * own_rows
    position = prefix_rows * devices + suffix_lengths
    own_position = lax.dynamic_slice_in_dim(position, row_start, own_rows, 0)
    own_lengths = lax.dynamic_slice_in_dim(suffix_lengths, row_start, own_rows, 0)
    attn_normed, local_normed = normalized_rows(tokens, attn_gain)
    query_width = q_weight.shape[1]
    query_cols = self_index * query_width + jnp.arange(query_width, dtype=jnp.int32)
    query_part = rotate(
        jnp.dot(attn_normed, q_weight, preferred_element_type=jnp.float32), position, query_cols
    ).astype(jnp.bfloat16)
    queries = lax.all_gather(query_part, "ctx", axis=1, tiled=True)
    key_width = k_weight.shape[1]
    key_term = jnp.dot(local_normed, k_weight, preferred_element_type=jnp.float32)
    value_term = jnp.dot(local_normed, v_weight, preferred_element_type=jnp.float32)
    fresh = lax.psum_scatter(
        jnp.concatenate([key_term, value_term], axis=1), "ctx", scatter_dimension=0, tiled=True
    )
    fresh_keys = rotate(
        fresh[:, :key_width], own_position, jnp.arange(key_width, dtype=jnp.int32)
    ).astype(jnp.bfloat16)
    fresh_values = fresh[:, key_width:].astype(jnp.bfloat16)
    query_heads = queries.reshape(samples, KV_HEADS, group_size, HEAD_DIM)
    head_keys = prefix_keys.reshape(prefix_rows, KV_HEADS, HEAD_DIM)
    head_values = prefix_values.reshape(prefix_rows, KV_HEADS, HEAD_DIM)
    scores = (
        jnp.einsum("sngd,tnd->sngt", query_heads, head_keys, preferred_element_type=jnp.float32)
        * score_scale
    )
    local_peak = jnp.max(scores, axis=-1)
    peak_heads = lax.pmax(local_peak, "ctx")
    weights = jnp.exp(scores - peak_heads[..., None])
    partial_total = jnp.sum(weights, axis=-1).reshape(samples, HEADS)
    summed = jnp.einsum(
        "sngt,tnd->sngd",
        weights.astype(jnp.bfloat16),
        head_values,
        preferred_element_type=jnp.float32,
    ).reshape(samples, HEADS * HEAD_DIM)
    every_sum, every_total = lax.psum((summed, partial_total), "ctx")
    prefix_sum = lax.dynamic_slice_in_dim(every_sum, row_start, own_rows, 0)
    prefix_total = lax.dynamic_slice_in_dim(every_total, row_start, own_rows, 0)
    prefix_peak = lax.dynamic_slice_in_dim(
        peak_heads.reshape(samples, HEADS), row_start, own_rows, 0
    )
    prefix_sum = prefix_sum.reshape(own_rows, HEADS, HEAD_DIM)
    own_queries = lax.dynamic_slice_in_dim(query_heads, row_start, own_rows, 0)
    suffix_span = suffix_table.shape[1] * suffix_keys.shape[1]
    owned_keys = suffix_keys[suffix_table].reshape(own_rows, suffix_span, KV_HEADS, HEAD_DIM)
    owned_values = suffix_values[suffix_table].reshape(own_rows, suffix_span, KV_HEADS, HEAD_DIM)
    every_key = jnp.concatenate(
        [owned_keys, fresh_keys.reshape(own_rows, 1, KV_HEADS, HEAD_DIM)], axis=1
    )
    every_value = jnp.concatenate(
        [owned_values, fresh_values.reshape(own_rows, 1, KV_HEADS, HEAD_DIM)], axis=1
    )
    slot_index = jnp.arange(suffix_span + 1, dtype=jnp.int32)
    live_mask = (slot_index[None, :] < own_lengths[:, None]) | (slot_index[None, :] == suffix_span)
    suffix_scores = (
        jnp.einsum("sngd,sjnd->sngj", own_queries, every_key, preferred_element_type=jnp.float32)
        * score_scale
    )
    suffix_scores = jnp.where(live_mask[:, None, None, :], suffix_scores, -1e30)
    suffix_peak = jnp.max(suffix_scores, axis=-1)
    suffix_weights = jnp.exp(suffix_scores - suffix_peak[..., None])
    suffix_total = jnp.sum(suffix_weights, axis=-1).reshape(own_rows, HEADS)
    suffix_sum = jnp.einsum(
        "sngj,sjnd->sngd",
        suffix_weights.astype(jnp.bfloat16),
        every_value,
        preferred_element_type=jnp.float32,
    ).reshape(own_rows, HEADS, HEAD_DIM)
    suffix_peak = suffix_peak.reshape(own_rows, HEADS)
    peak_all = jnp.maximum(prefix_peak, suffix_peak)
    prefix_factor = jnp.exp(prefix_peak - peak_all)
    suffix_factor = jnp.exp(suffix_peak - peak_all)
    numerator = prefix_sum * prefix_factor[..., None] + suffix_sum * suffix_factor[..., None]
    denominator = prefix_total * prefix_factor + suffix_total * suffix_factor
    attention = (
        (numerator / denominator[..., None])
        .reshape(own_rows, HEADS * HEAD_DIM)
        .astype(jnp.bfloat16)
    )
    attended = jnp.dot(
        lax.all_gather(attention, "ctx", axis=0, tiled=True),
        o_weight,
        preferred_element_type=jnp.float32,
    )
    mixed_rows = (tokens.astype(jnp.float32) + attended).astype(jnp.bfloat16)
    mlp_normed = normalized_rows(mixed_rows, mlp_gain)[0]
    gate_proj = jnp.dot(mlp_normed, gate_weight, preferred_element_type=jnp.float32)
    up_proj = jnp.dot(mlp_normed, up_weight, preferred_element_type=jnp.float32)
    hidden = (jax.nn.silu(gate_proj) * up_proj).astype(jnp.bfloat16)
    partial_value = jnp.dot(hidden, down_weight, preferred_element_type=jnp.float32)
    shares = lax.psum_scatter(partial_value, "ctx", scatter_dimension=1, tiled=True)
    return (mixed_rows.astype(jnp.float32) + shares).astype(jnp.bfloat16)


def solution(mesh):
    placed = (
        P("groups", "ctx"),
        P(),
        P(),
        P(None, "ctx"),
        P("ctx", None),
        P("ctx", None),
        P(None, "ctx"),
        P(None, "ctx"),
        P(None, "ctx"),
        P("ctx", None),
        P(("groups", "ctx"), None),
        P(("groups", "ctx"), None),
        P(("groups", "ctx"), None, None),
        P(("groups", "ctx"), None, None),
        P("groups"),
        P(("groups", "ctx"), None),
    )
    return jax.shard_map(
        body, mesh=mesh, in_specs=placed, out_specs=P("groups", "ctx"), check_vma=False
    )
```

profile of v0, /device:TPU:0, one launch (start us, length us, event | category | flops | bytes accessed | tf_op | source)
XLA Modules:
  0.0 365.9 jit_solution(18179177284620579872)
XLA Ops:
  6.5 24.2 %all_gather.12 = bf16[16,8192]{1,0:T(8,128)(2,1)S(1)} all-gather(bf16[16,512]{1,0:T(8,128)(2,1)} %param.16), channel_id=1, replica_groups=mesh['groups'=2,'ctx'=16] {'ctx'}, dimensions={1}, use_global_device_ids=true | all-gather | bytes 278528 | tf_op jit(solution)/shard_map/all_gather | solution.py:33
  30.9 0.9 fusion.9
  31.8 4.6 %fusion.70 = f32[16,512]{1,0:T(8,128)S(1)} fusion(bf16[16,8192]{1,0:T(8,128)(2,1)S(1)} %fusion.9, bf16[8192,512]{1,0:T(8,128)(2,1)} %param.19), kind=kOutput, calls=%fused_computation.119 | convolution fusion | flops 134217728 | bytes 8683520 | tf_op jit(solution)/shard_map/dot_general | solution.py:74
  39.1 30.1 %all_gather.13 = bf16[16,8192]{0,1:T(8,128)(2,1)S(1)} all-gather(bf16[16,512]{0,1:T(8,128)(2,1)S(1)} %bitcast.91), channel_id=1, replica_groups=mesh['groups'=2,'ctx'=16] {'ctx'}, dimensions={1}, use_global_device_ids=true | all-gather | bytes 278528 | tf_op jit(solution)/shard_map/all_gather | solution.py:76
  69.2 1.5 copy.68
  70.6 1.1 copy.91
  71.8 2.3 fusion.68
  74.0 60.5 %pmax.7 = f32[16,8,8]{2,0,1:T(8,128)S(1)} all-reduce(f32[16,8,8]{2,0,1:T(8,128)S(1)} %get-tuple-element.20), channel_id=1, replica_groups=mesh['groups'=2,'ctx'=16] {'ctx'}, use_global_device_ids=true, to_apply=%region_2.3 | all-reduce | flops 1024 | bytes 8192 | tf_op jit(solution)/shard_map/pmax | solution.py:95
  134.6 1.1 copy.92
  135.7 1.6 convolution_bitcast_fusion
  137.4 1.1 copy.107
  138.7 1.5 fusion.41
  141.0 2.0 constant_dynamic-slice_fusion.1
  143.0 1.2 dynamic_slice.23
  144.2 1.6 fusion.4
  145.9 1.3 dynamic_slice.26
  148.1 2.0 copy.90
  150.1 0.7 fusion.58
  150.7 1.5 gather_fusion
  152.4 1.5 gather_fusion.1
  154.1 30.1 %psum.15 = f32[16,64]{1,0:T(8,128)S(1)} all-reduce(f32[16,64]{1,0:T(8,128)S(1)} %copy.79), channel_id=1, replica_groups=mesh['groups'=2,'ctx'=16] {'ctx'}, use_global_device_ids=true, to_apply=%region_7.8 | all-reduce | flops 1024 | bytes 8192 | tf_op jit(solution)/shard_map/psum | solution.py:104
  185.6 44.7 %all-reduce.4.cloned.1.call-done = (f32[16,2048]{1,0:T(8,128)}, f32[16,8192]{1,0:T(8,128)}) async-done(((f32[16,2048]{1,0:T(8,128)}, f32[16,8192]{1,0:T(8,128)}), (f32[16,2048]{1,0:T(8,128)}, f32[16,8192]{1,0:T(8,128)})) %all-reduce.4.cloned.1.call-update) | async-done | bytes 655376
  230.3 1.4 constant_dynamic-slice_fusion.3
  232.6 1.5 fusion.45
  235.3 1.0 convert_bitcast_fusion
  236.3 21.7 %all-gather = bf16[16,1,8192]{2,1,0:T(2,128)(2,1)S(1)} all-gather(bf16[1,1,8192]{2,1,0:T(2,128)(2,1)S(1)} %convert_bitcast_fusion), channel_id=1, replica_groups=mesh['groups'=2,'ctx'=16] {'ctx'}, dimensions={0}, use_global_device_ids=true | all-gather | bytes 278528 | tf_op jit(solution)/shard_map/all_gather | solution.py:149
  258.0 4.6 %fusion.3 = bf16[16,512]{1,0:T(8,128)(2,1)S(1)} fusion(bf16[8192,512]{1,0:T(8,128)(2,1)} %param.22, bf16[16,1,8192]{2,1,0:T(2,128)(2,1)S(1)} %all-gather, bf16[16,512]{1,0:T(8,128)(2,1)S(1)} %copy-done.3), kind=kOutput, calls=%fused_computation.10 | convolution fusion | flops 134242304 | bytes 8683520 | tf_op jit(solution)/shard_map/dot_general | solution.py:148
  262.5 18.3 %all_gather.15 = bf16[16,8192]{1,0:T(8,128)(2,1)S(1)} all-gather(bf16[16,512]{1,0:T(8,128)(2,1)S(1)} %fusion.3), channel_id=1, replica_groups=mesh['groups'=2,'ctx'=16] {'ctx'}, dimensions={1}, use_global_device_ids=true | all-gather | bytes 278528 | tf_op jit(solution)/shard_map/all_gather | solution.py:33
  281.1 8.2 %fusion.31 = f32[16,1024]{1,0:T(8,128)S(1)} fusion(bf16[8192,1024]{1,0:T(8,128)(2,1)} %param.23, bf16[16,8192]{1,0:T(8,128)(2,1)S(1)} %all_gather.15, f32[8192]{0:T(1024)S(1)} %copy-done.2, f32[16]{0:T(128)S(1)} %add_rsqrt_fusion), kind=kOutput, calls=%fused_computation.45 | convolution fusion | flops 268959744 | bytes 17137728 | tf_op jit(solution)/shard_map/dot_general | solution.py:155
  289.2 13.7 %fusion.6 = f32[16,8192]{1,0:T(8,128)} fusion(bf16[1024,8192]{1,0:T(8,128)(2,1)} %param.25, bf16[8192,1024]{1,0:T(8,128)(2,1)} %param.24, f32[16,1024]{1,0:T(8,128)S(1)} %fusion.31, bf16[16,8192]{1,0:T(8,128)(2,1)S(1)} %all_gather.15, f32[8192]{0:T(1024)S(1)} %copy-done.2, f32[16]{0:T(128)S(1)} %add_rsqrt_fusion), kind=kOutput, calls=%fused_computation.18 | convolution fusion | flops 537493504 | bytes 34439232 | tf_op jit(solution)/shard_map/dot_general | solution.py:158
  303.0 54.7 %reduce-scatter.2.cloned.1.call-done = f32[16,512]{1,0:T(8,128)} async-done(((f32[16,8192]{1,0:T(8,128)}), f32[16,512]{1,0:T(8,128)}) %reduce-scatter.2.cloned.1.call-update) | async-done | bytes 32784 | tf_op jit(solution)/shard_map/reduce_scatter | solution.py:159
  357.7 1.4 add_convert_fusion
  (63 shorter events, 8.1 us)
Async XLA Ops:
  6.5 132.0 %copy-start = (bf16[512,1024]{1,0:T(8,128)(2,1)S(1)}, bf16[512,1024]{1,0:T(8,128)(2,1)}, u32[]{:S(2)}) copy-start(bf16[512,1024]{1,0:T(8,128)(2,1)} %param.21) | copy-start | bytes 3145732
  6.5 31.1 %copy-start.4 = (s32[16]{0:T(128)S(1)}, s32[16]{0:T(128)}, u32[]{:S(2)}) copy-start(s32[16]{0:T(128)} %param.30) | copy-start | bytes 196
  6.5 223.8 %all-reduce.4.cloned.1.call-start = ((), (), s32[]{:S(2)}) async-start(), calls=%async_computation.2 | async-start | bytes 1310720
  36.4 221.6 %copy-start.3 = (bf16[16,512]{1,0:T(8,128)(2,1)S(1)}, bf16[16,512]{1,0:T(8,128)(2,1)}, u32[]{:S(2)}) copy-start(bf16[16,512]{1,0:T(8,128)(2,1)} %param.16) | copy-start | bytes 49156
  134.6 49.8 %copy-start.5 = (u32[32]{0:T(128)S(1)}, u32[32]{0:T(128)}, u32[]{:S(2)}) copy-start(u32[32]{0:T(128)} %constant.89) | copy-start | bytes 388
  134.6 146.5 %copy-start.2 = (f32[8192]{0:T(1024)S(1)}, f32[8192]{0:T(1024)}, u32[]{:S(2)}) copy-start(f32[8192]{0:T(1024)} %param.18) | copy-start | bytes 98308
  140.9 216.8 %reduce-scatter.2.cloned.1.call-start = ((), (), s32[]{:S(2)}) async-start(), calls=%async_computation.1 | async-start | bytes 557056 | tf_op jit(solution)/shard_map/reduce_scatter | solution.py:159
  281.1 78.0 %copy-start.1 = (bf16[512,1024]{1,0:T(8,128)(2,1)S(1)}, bf16[512,1024]{1,0:T(8,128)(2,1)}, u32[]{:S(2)}) copy-start(bf16[512,1024]{1,0:T(8,128)(2,1)} %param.21) | copy-start | bytes 3145732
Sparse Core Ops, SparseCore 0:
  141.0 89.2 all-reduce.3
  303.1 54.5 reduce-scatter.1
where the time goes:
time: 367 us; the launch traced here: 366 us
  blocking collectives  185 us (50%)
  waiting for transfers between devices  99.5 us (27%)
  matrix products  37.2 us (10%)
  local copies, waits for them, and re-layouts  22 us (6%)
  between operations  14.3 us (4%)
  other arithmetic  8.09 us (2%)
    pmax x1, blocking collectives, body(): peak_heads = lax.pmax(local_peak, 'ctx')  60.5 us
    reduce_scatter x1, waiting for transfers between devices, body(): lax.psum_scatter(partial_value, 'ctx', scatter_dimension=1, tiled=True)  54.7 us
    unnamed x3, waiting for transfers between devices  44.7 us
    all_gather x2, blocking collectives, normalized_rows(): gathered_raw = lax.all_gather(shard_rows, 'ctx', axis=1, tiled=True)  42.5 us
    psum x1, blocking collectives, body(): every_sum, every_total = lax.psum((summed, partial_total), 'ctx')  30.1 us
    all_gather x1, blocking collectives, body(): queries = lax.all_gather(query_part, 'ctx', axis=1, tiled=True)  30.1 us
    all_gather x1, blocking collectives, body(): lax.all_gather(attention, 'ctx', axis=0, tiled=True)  21.7 us
    dot_general x1, matrix products, body(): jnp.dot(hidden, down_weight, preferred_element_type=jnp.float32)  13.7 us
  transfers between devices with their start and end apart: 2, of which 2 were waited for; matrix products, arithmetic and copies ran while one was open for 4% of the time, Pallas kernels for 0%

commit v1 on v0

v1 whole, which is shorter than its diff:
```python
import math

import jax
import jax.numpy as jnp
from jax import lax
from jax.sharding import PartitionSpec as P

HEADS = 64
KV_HEADS = 8
HEAD_DIM = 128


EPSILON = 1e-05
ROPE_BASE = 500000.0


def rotate(matrix, position, columns):
    pair_index = (columns % HEAD_DIM // 2).astype(jnp.float32)
    frequency = jnp.exp(pair_index * (-2.0 * math.log(ROPE_BASE) / HEAD_DIM))
    angles = position.astype(jnp.float32)[:, None] * frequency[None, :]
    cosine = jnp.cos(angles[:, 0::2])
    sine_part = jnp.sin(angles[:, 0::2])
    even_part = matrix[:, 0::2]
    odd_part = matrix[:, 1::2]
    rotated_even = even_part * cosine - odd_part * sine_part
    rotated_odd = even_part * sine_part + odd_part * cosine
    return jnp.stack([rotated_even, rotated_odd], axis=-1).reshape(matrix.shape)


def exchange(blocks):
    return lax.all_to_all(blocks, "ctx", 0, 0, tiled=True)


def gather_blocks(block):
    devices = lax.axis_size("ctx")
    return exchange(jnp.broadcast_to(block[None], (devices,) + block.shape))


def split_pieces(value, count):
    pieces = []
    rest = value
    for _ in range(count):
        piece = lax.reduce_precision(rest, 8, 7)
        pieces.append(piece.astype(jnp.bfloat16))
        rest = rest - piece
    return pieces


def normalized(blocks, gain_vector):
    devices, samples, width = blocks.shape
    widened = blocks.astype(jnp.float32)
    mean_square = jnp.sum(widened * widened, axis=(0, 2), keepdims=True) / (devices * width)
    scaled = widened * lax.rsqrt(mean_square + EPSILON) * gain_vector.reshape(devices, 1, width)
    return scaled.astype(jnp.bfloat16)


def columns_dot(blocks, weight):
    devices, samples, width = blocks.shape
    rows = blocks.transpose(1, 0, 2).reshape(samples, devices * width)
    return jnp.dot(rows, weight, preferred_element_type=jnp.float32)


def body(
    tokens,
    attn_gain,
    mlp_gain,
    q_weight,
    k_weight,
    v_weight,
    o_weight,
    gate_weight,
    up_weight,
    down_weight,
    prefix_keys,
    prefix_values,
    suffix_keys,
    suffix_values,
    suffix_lengths,
    suffix_table,
):
    self_index = lax.axis_index("ctx")
    devices = lax.axis_size("ctx")
    samples, width = tokens.shape
    own_rows = suffix_table.shape[0]
    group_size = HEADS // KV_HEADS
    score_scale = 1.0 / math.sqrt(HEAD_DIM)
    prefix_rows = prefix_keys.shape[0]
    row_start = self_index * own_rows
    position = prefix_rows * devices + suffix_lengths
    own_position = lax.dynamic_slice_in_dim(position, row_start, own_rows, 0)
    own_lengths = lax.dynamic_slice_in_dim(suffix_lengths, row_start, own_rows, 0)
    attn_normed = normalized(gather_blocks(tokens), attn_gain)
    local_normed = lax.dynamic_index_in_dim(attn_normed, self_index, 0, keepdims=False)
    query_width = q_weight.shape[1]
    query_cols = self_index * query_width + jnp.arange(query_width, dtype=jnp.int32)
    query_part = rotate(columns_dot(attn_normed, q_weight), position, query_cols).astype(
        jnp.bfloat16
    )
    key_width = k_weight.shape[1]
    key_term = jnp.dot(local_normed, k_weight, preferred_element_type=jnp.float32)
    value_term = jnp.dot(local_normed, v_weight, preferred_element_type=jnp.float32)
    fresh_high, fresh_low = split_pieces(jnp.concatenate([key_term, value_term], axis=1), 2)
    fresh_part = jnp.concatenate([fresh_high, fresh_low], axis=1).reshape(devices, -1)
    payload = jnp.concatenate(
        [jnp.broadcast_to(query_part.reshape(1, -1), (devices, query_part.size)), fresh_part],
        axis=1,
    ).reshape(devices, -1, HEAD_DIM)
    received = exchange(payload).reshape(devices, -1)
    queries = received[:, : query_part.size].reshape(devices, samples, query_width)
    queries = queries.transpose(1, 0, 2).reshape(samples, devices * query_width)
    fresh = received[:, query_part.size :].astype(jnp.float32)
    fresh = jnp.sum(fresh, axis=0).reshape(own_rows, 2, 2 * key_width)
    fresh = fresh[:, 0] + fresh[:, 1]
    fresh_keys = rotate(
        fresh[:, :key_width], own_position, jnp.arange(key_width, dtype=jnp.int32)
    ).astype(jnp.bfloat16)
    fresh_values = fresh[:, key_width:].astype(jnp.bfloat16)
    query_heads = queries.reshape(samples, KV_HEADS, group_size, HEAD_DIM)
    head_keys = prefix_keys.reshape(prefix_rows, KV_HEADS, HEAD_DIM)
    head_values = prefix_values.reshape(prefix_rows, KV_HEADS, HEAD_DIM)
    scores = (
        jnp.einsum("sngd,tnd->sngt", query_heads, head_keys, preferred_element_type=jnp.float32)
        * score_scale
    )
    local_peak = jnp.max(scores, axis=-1)
    weights = jnp.exp(scores - local_peak[..., None])
    local_total = jnp.sum(weights, axis=-1).reshape(samples, HEADS)
    local_peak = local_peak.reshape(samples, HEADS)
    local_sum = jnp.einsum(
        "sngt,tnd->sngd",
        weights.astype(jnp.bfloat16),
        head_values,
        preferred_element_type=jnp.float32,
    ).reshape(samples, HEADS * HEAD_DIM)
    stats = jnp.concatenate(split_pieces(local_peak, 3) + split_pieces(local_total, 3), axis=1)
    parts = jnp.concatenate([local_sum.astype(jnp.bfloat16), stats], axis=1)
    parts = exchange(parts.reshape(devices, own_rows, -1)).astype(jnp.float32)
    every_sum = parts[:, :, : HEADS * HEAD_DIM].reshape(devices, own_rows, HEADS, HEAD_DIM)
    stats = parts[:, :, HEADS * HEAD_DIM :].reshape(devices, own_rows, 2, 3, HEADS)
    stats = (stats[:, :, :, 0] + stats[:, :, :, 1]) + stats[:, :, :, 2]
    every_peak = stats[:, :, 0]
    every_total = stats[:, :, 1]
    own_queries = lax.dynamic_slice_in_dim(query_heads, row_start, own_rows, 0)
    blocks, block_size = suffix_keys.shape[:2]
    table_places = suffix_table.shape[1]
    owned_keys = suffix_keys.reshape(blocks * block_size, KV_HEADS, HEAD_DIM)
    owned_values = suffix_values.reshape(blocks * block_size, KV_HEADS, HEAD_DIM)
    places = jnp.arange(table_places, dtype=jnp.int32)
    held = suffix_table[:, :, None] == jnp.arange(blocks, dtype=jnp.int32)
    limit = jnp.where(held, own_lengths[:, None, None] - places[:, None] * block_size, 0)
    limit = jnp.max(limit, axis=1)
    live_mask = jnp.arange(block_size, dtype=jnp.int32) < limit[:, :, None]
    live_mask = live_mask.reshape(own_rows, 1, 1, blocks * block_size)
    slot_scores = (
        jnp.einsum("sngd,jnd->sngj", own_queries, owned_keys, preferred_element_type=jnp.float32)
        * score_scale
    )
    slot_scores = jnp.where(live_mask, slot_scores, -1e30)
    fresh_scores = score_scale * jnp.sum(
        own_queries.astype(jnp.float32)
        * fresh_keys.astype(jnp.float32).reshape(own_rows, KV_HEADS, 1, HEAD_DIM),
        axis=-1,
    )
    suffix_peak = jnp.maximum(jnp.max(slot_scores, axis=-1), fresh_scores)
    slot_weights = jnp.exp(slot_scores - suffix_peak[..., None])
    fresh_weights = jnp.exp(fresh_scores - suffix_peak)
    suffix_total = (jnp.sum(slot_weights, axis=-1) + fresh_weights).reshape(own_rows, HEADS)
    suffix_sum = jnp.einsum(
        "sngj,jnd->sngd",
        slot_weights.astype(jnp.bfloat16),
        owned_values,
        preferred_element_type=jnp.float32,
    )
    suffix_sum = suffix_sum + lax.reduce_precision(fresh_weights, 8, 7)[
        ..., None
    ] * fresh_values.astype(jnp.float32).reshape(own_rows, KV_HEADS, 1, HEAD_DIM)
    suffix_sum = suffix_sum.reshape(own_rows, HEADS, HEAD_DIM)
    suffix_peak = suffix_peak.reshape(own_rows, HEADS)
    peak_all = jnp.maximum(jnp.max(every_peak, axis=0), suffix_peak)
    part_factor = jnp.exp(every_peak - peak_all)
    suffix_factor = jnp.exp(suffix_peak - peak_all)
    numerator = (
        jnp.sum(every_sum * part_factor[..., None], axis=0) + suffix_sum * suffix_factor[..., None]
    )
    denominator = jnp.sum(every_total * part_factor, axis=0) + suffix_total * suffix_factor
    attention = (
        (numerator / denominator[..., None])
        .reshape(own_rows * HEADS, HEAD_DIM)
        .astype(jnp.bfloat16)
    )
    attention = gather_blocks(attention).reshape(samples, HEADS * HEAD_DIM)
    attended = jnp.dot(attention, o_weight, preferred_element_type=jnp.float32)
    mixed_rows = (tokens.astype(jnp.float32) + attended).astype(jnp.bfloat16)
    mlp_normed = normalized(gather_blocks(mixed_rows), mlp_gain)
    mlp_normed = mlp_normed.transpose(1, 0, 2).reshape(samples, devices * width)
    gate_proj = jnp.dot(mlp_normed, gate_weight, preferred_element_type=jnp.float32)
    up_proj = jnp.dot(mlp_normed, up_weight, preferred_element_type=jnp.float32)
    hidden = (jax.nn.silu(gate_proj) * up_proj).astype(jnp.bfloat16)
    partial_value = jnp.dot(hidden, down_weight, preferred_element_type=jnp.float32)
    partial_value = partial_value.astype(jnp.bfloat16).reshape(samples, devices, width)
    shares = exchange(partial_value.transpose(1, 0, 2))
    shares = jnp.sum(shares.astype(jnp.float32), axis=0)
    return (mixed_rows.astype(jnp.float32) + shares).astype(jnp.bfloat16)


def solution(mesh):
    placed = (
        P("groups", "ctx"),
        P(),
        P(),
        P(None, "ctx"),
        P("ctx", None),
        P("ctx", None),
        P(None, "ctx"),
        P(None, "ctx"),
        P(None, "ctx"),
        P("ctx", None),
        P(("groups", "ctx"), None),
        P(("groups", "ctx"), None),
        P(("groups", "ctx"), None, None),
        P(("groups", "ctx"), None, None),
        P("groups"),
        P(("groups", "ctx"), None),
    )
    return jax.shard_map(
        body, mesh=mesh, in_specs=placed, out_specs=P("groups", "ctx"), check_vma=False
    )
```

time: 367 us -> 134 us (0.37)
  blocking collectives: 185 us -> 25.5 us
  waiting for transfers between devices: 99.5 us -> 31.9 us
  starting transfers between devices: 0.04 us -> 18 us
  between operations: 14.3 us -> 1.13 us
  matrix products: 37.2 us -> 32 us
    all_gather x4 -> x0, blocking collectives: 94.2 us -> none  [the longest x2 42.5 us: normalized_rows(): gathered_raw = lax.all_gather(shard_rows, 'ctx', axis=1, tiled=True)]
    pmax x1 -> x0, blocking collectives: 60.5 us -> none  [body(): peak_heads = lax.pmax(local_peak, 'ctx')]
    reduce_scatter x1 -> x0, waiting for transfers between devices: 54.7 us -> none  [body(): lax.psum_scatter(partial_value, 'ctx', scatter_dimension=1, tiled=True)]
    unnamed x3 -> x0, waiting for transfers between devices: 44.7 us -> none
    all_to_all x0 -> x4, waiting for transfers between devices: none -> 31.9 us  [exchange(): return lax.all_to_all(blocks, 'ctx', 0, 0, tiled=True)]
    psum x1 -> x0, blocking collectives: 30.1 us -> none  [body(): every_sum, every_total = lax.psum((summed, partial_total), 'ctx')]
    all_to_all x0 -> x2, blocking collectives: none -> 25.5 us  [exchange(): return lax.all_to_all(blocks, 'ctx', 0, 0, tiled=True)]
    all_to_all x0 -> x4, starting transfers between devices: none -> 18 us  [exchange(): return lax.all_to_all(blocks, 'ctx', 0, 0, tiled=True)]
  transfers between devices with their start and end apart: 2 -> 4, of which waited for: 2 -> 4; matrix products, arithmetic and copies ran while one was open for 4% -> 7% of each run, Pallas kernels for 0% -> 0%
where the time goes in v1:
time: 134 us; the launch traced here: 133 us
  matrix products  32 us (24%)
  waiting for transfers between devices  31.9 us (24%)
  blocking collectives  25.5 us (19%)
  local copies, waits for them, and re-layouts  18.6 us (14%)
  starting transfers between devices  18 us (13%)
  other arithmetic  5.91 us (4%)
    all_to_all x4, waiting for transfers between devices, exchange(): return lax.all_to_all(blocks, 'ctx', 0, 0, tiled=True)  31.9 us
    all_to_all x2, blocking collectives, exchange(): return lax.all_to_all(blocks, 'ctx', 0, 0, tiled=True)  25.5 us
    all_to_all x4, starting transfers between devices, exchange(): return lax.all_to_all(blocks, 'ctx', 0, 0, tiled=True)  18 us
    dot_general x1, matrix products, body(): jnp.dot(hidden, down_weight, preferred_element_type=jnp.float32)  12.9 us
    dot_general x1, matrix products, body(): jnp.dot(mlp_normed, gate_weight, preferred_element_type=jnp.float32)  8.13 us
    unnamed x24, local copies, waits for them, and re-layouts  6.96 us
    dot_general x1, matrix products, body(): attended = jnp.dot(attention, o_weight, preferred_element_type=jnp.float32)  4.56 us
    dot_general x1, matrix products, columns_dot(): return jnp.dot(rows, weight, preferred_element_type=jnp.float32)  4.56 us
  transfers between devices with their start and end apart: 4, of which 4 were waited for; matrix products, arithmetic and copies ran while one was open for 7% of the time, Pallas kernels for 0%

profile of v1, /device:TPU:0, one launch (start us, length us, event | category | flops | bytes accessed | tf_op | source)
XLA Modules:
  0.0 133.0 jit_solution(7327029711099846360)
XLA Ops:
  0.0 1.6 %broadcast_in_dim.28 = bf16[16,16,512]{2,1,0:T(8,128)(2,1)} broadcast(bf16[16,512]{1,0:T(8,128)(2,1)} %param.16), dimensions={1,2} | broadcast | bytes 278528 | tf_op jit(solution)/shard_map/broadcast_in_dim | solution.py:36
  1.6 7.4 %all-to-all-start = ((bf16[16,16,512]{2,1,0:T(8,128)(2,1)}), bf16[16,16,512]{2,1,0:T(8,128)(2,1)S(1)}, u32[]{:S(2)}, u32[]{:S(2)}) async-start(bf16[16,16,512]{2,1,0:T(8,128)(2,1)} %broadcast_in_dim.28), calls=%async_computation | async-start | bytes 524288 | tf_op jit(solution)/shard_map/all_to_all | solution.py:31
  9.0 0.7 broadcast_add_fusion
  9.7 0.8 mul.289
  10.6 0.6 slice.61
  11.2 7.8 %all-to-all-done = bf16[16,16,512]{2,1,0:T(8,128)(2,1)S(1)} async-done(((bf16[16,16,512]{2,1,0:T(8,128)(2,1)}), bf16[16,16,512]{2,1,0:T(8,128)(2,1)S(1)}, u32[]{:S(2)}, u32[]{:S(2)}) %all-to-all-start) | async-done | bytes 262176 | tf_op jit(solution)/shard_map/all_to_all | solution.py:31
  19.4 4.6 %fusion.78 = f32[16,512]{1,0:T(8,128)S(1)} fusion(bf16[16,8192]{1,0:T(8,128)(2,1)S(1)} %bitcast.145, bf16[8192,512]{1,0:T(8,128)(2,1)} %param.19), kind=kOutput, calls=%fused_computation.147 | convolution fusion | flops 134217728 | bytes 8683520 | tf_op jit(solution)/shard_map/dot_general | solution.py:60
  24.0 0.6 slice.60
  24.6 0.6 slice.62
  25.8 1.6 %reshape.691 = bf16[8192]{0:T(1024)(128)(2,1)S(1)} reshape(bf16[16,256,2]{2,1,0:T(8,128)(2,1)S(1)} %copy.73) | data formatting | bytes 32768 | tf_op jit(solution)/shard_map/convert_element_type | solution.py:96
  28.1 0.8 copy.102
  28.9 3.6 %all-to-all-start.1 = ((bf16[16,96,128]{2,1,0:T(8,128)(2,1)}), bf16[16,96,128]{2,1,0:T(8,128)(2,1)S(1)}, u32[]{:S(2)}, u32[]{:S(2)}) async-start(bf16[16,96,128]{2,1,0:T(8,128)(2,1)} %bitcast.49), calls=%async_computation.1 | async-start | bytes 786432 | tf_op jit(solution)/shard_map/all_to_all | solution.py:31
  33.0 0.6 dynamic_slice.16
  34.6 0.7 multiply_subtract_fusion
  35.6 1.0 copy.108
  36.6 1.1 copy.105
  37.7 1.1 copy.106
  38.8 1.0 copy.109
  39.9 4.6 %all-to-all-done.1 = bf16[16,96,128]{2,1,0:T(8,128)(2,1)S(1)} async-done(((bf16[16,96,128]{2,1,0:T(8,128)(2,1)}), bf16[16,96,128]{2,1,0:T(8,128)(2,1)S(1)}, u32[]{:S(2)}, u32[]{:S(2)}) %all-to-all-start.1) | async-done | bytes 393248 | tf_op jit(solution)/shard_map/all_to_all | solution.py:31
  48.5 0.8 reduce.11
  49.4 1.0 reshape.692
  50.3 3.5 %all-to-all-start.2 = ((bf16[16,2,4288]{2,1,0:T(2,128)(2,1)}), bf16[16,2,4288]{2,1,0:T(2,128)(2,1)S(1)}, u32[]{:S(2)}, u32[]{:S(2)}) async-start(bf16[16,2,4288]{2,1,0:T(2,128)(2,1)} %reshape.692), calls=%async_computation.2 | async-start | bytes 557056 | tf_op jit(solution)/shard_map/all_to_all | solution.py:31
  54.6 9.5 %all-to-all-done.2 = bf16[16,2,4288]{2,1,0:T(2,128)(2,1)S(1)} async-done(((bf16[16,2,4288]{2,1,0:T(2,128)(2,1)}), bf16[16,2,4288]{2,1,0:T(2,128)(2,1)S(1)}, u32[]{:S(2)}, u32[]{:S(2)}) %all-to-all-start.2) | async-done | bytes 274464 | tf_op jit(solution)/shard_map/all_to_all | solution.py:31
  66.6 12.8 %all_to_all.30 = bf16[16,64,128]{2,1,0:T(8,128)(2,1)S(1)} all-to-all(bf16[16,64,128]{2,1,0:T(8,128)(2,1)S(1)} %broadcast_in_dim.38), channel_id=1, replica_groups=mesh['groups'=2,'ctx'=16] {'ctx'}, dimensions={0} | all-to-all | bytes 524288 | tf_op jit(solution)/shard_map/all_to_all | solution.py:31
  79.3 4.6 %fusion.11 = bf16[16,512]{1,0:T(8,128)(2,1)S(1)} fusion(bf16[8192,512]{1,0:T(8,128)(2,1)} %param.22, bf16[2,8,64,128]{3,2,1,0:T(8,128)(2,1)S(1)} %bitcast.146, bf16[16,512]{1,0:T(8,128)(2,1)S(1)} %copy-done.3), kind=kOutput, calls=%fused_computation.18 | convolution fusion | flops 134242304 | bytes 8683520 | tf_op jit(solution)/shard_map/dot_general | solution.py:192
  83.9 0.7 broadcast_in_dim.39
  84.6 3.5 %all-to-all-start.4 = ((bf16[16,16,512]{2,1,0:T(8,128)(2,1)}), bf16[16,16,512]{2,1,0:T(8,128)(2,1)S(1)}, u32[]{:S(2)}, u32[]{:S(2)}) async-start(bf16[16,16,512]{2,1,0:T(8,128)(2,1)} %broadcast_in_dim.39), calls=%async_computation.4 | async-start | bytes 524288 | tf_op jit(solution)/shard_map/all_to_all | solution.py:31
  88.2 10.0 %all-to-all-done.4 = bf16[16,16,512]{2,1,0:T(8,128)(2,1)S(1)} async-done(((bf16[16,16,512]{2,1,0:T(8,128)(2,1)}), bf16[16,16,512]{2,1,0:T(8,128)(2,1)S(1)}, u32[]{:S(2)}, u32[]{:S(2)}) %all-to-all-start.4) | async-done | bytes 262176 | tf_op jit(solution)/shard_map/all_to_all | solution.py:31
  98.5 8.1 %fusion.79 = f32[16,1024]{1,0:T(8,128)S(1)} fusion(bf16[16,8192]{1,0:T(8,128)(2,1)S(1)} %bitcast.143, bf16[8192,1024]{1,0:T(8,128)(2,1)} %param.23), kind=kOutput, calls=%fused_computation.148 | convolution fusion | flops 268435456 | bytes 17104896 | tf_op jit(solution)/shard_map/dot_general | solution.py:196
  106.7 12.9 %convolution_convert_fusion = bf16[16,8192]{1,0:T(8,128)(2,1)S(1)} fusion(bf16[1024,8192]{1,0:T(8,128)(2,1)} %param.25, bf16[16,8192]{1,0:T(8,128)(2,1)S(1)} %bitcast.144, bf16[8192,1024]{1,0:T(8,128)(2,1)} %param.24, f32[16,1024]{1,0:T(8,128)S(1)} %fusion.79), kind=kOutput, calls=%fused_computation | convolution fusion | flops 537100288 | bytes 34144256 | tf_op jit(solution)/shard_map/dot_general | solution.py:199
  119.7 12.7 %all_to_all.31 = bf16[16,16,512]{2,1,0:T(8,128)(2,1)S(1)} all-to-all(bf16[16,16,512]{2,1,0:T(8,128)(2,1)S(1)} %bitcast.160), channel_id=1, replica_groups=mesh['groups'=2,'ctx'=16] {'ctx'}, dimensions={0} | all-to-all | bytes 524288 | tf_op jit(solution)/shard_map/all_to_all | solution.py:31
  132.4 0.6 add_convert_fusion
  (97 shorter events, 10.4 us)
Async XLA Ops:
  0.0 27.5 %copy-start = (bf16[512,1024]{1,0:T(8,128)(2,1)S(1)}, bf16[512,1024]{1,0:T(8,128)(2,1)}, u32[]{:S(2)}) copy-start(bf16[512,1024]{1,0:T(8,128)(2,1)} %param.21) | copy-start | bytes 3145732
  0.0 32.4 %copy-start.5 = (s32[16]{0:T(128)S(1)}, s32[16]{0:T(128)}, u32[]{:S(2)}) copy-start(s32[16]{0:T(128)} %param.30) | copy-start | bytes 196
  0.0 27.7 %copy-start.2 = (bf16[512,1024]{1,0:T(8,128)(2,1)S(1)}, bf16[512,1024]{1,0:T(8,128)(2,1)}, u32[]{:S(2)}) copy-start(bf16[512,1024]{1,0:T(8,128)(2,1)} %param.20) | copy-start | bytes 3145732
  0.0 35.2 %copy-start.6 = (s32[1,8]{1,0:T(1,128)S(1)}, s32[1,8]{1,0:T(1,128)}, u32[]{:S(2)}) copy-start(s32[1,8]{1,0:T(1,128)} %param.31) | copy-start | bytes 100
  1.6 17.4 %all-to-all-start = ((bf16[16,16,512]{2,1,0:T(8,128)(2,1)}), bf16[16,16,512]{2,1,0:T(8,128)(2,1)S(1)}, u32[]{:S(2)}, u32[]{:S(2)}) async-start(bf16[16,16,512]{2,1,0:T(8,128)(2,1)} %broadcast_in_dim.28), calls=%async_computation | async-start | bytes 524288 | tf_op jit(solution)/shard_map/all_to_all | solution.py:31
  24.0 55.4 %copy-start.3 = (bf16[16,512]{1,0:T(8,128)(2,1)S(1)}, bf16[16,512]{1,0:T(8,128)(2,1)}, u32[]{:S(2)}) copy-start(bf16[16,512]{1,0:T(8,128)(2,1)} %param.16) | copy-start | bytes 49156
  28.9 15.7 %all-to-all-start.1 = ((bf16[16,96,128]{2,1,0:T(8,128)(2,1)}), bf16[16,96,128]{2,1,0:T(8,128)(2,1)S(1)}, u32[]{:S(2)}, u32[]{:S(2)}) async-start(bf16[16,96,128]{2,1,0:T(8,128)(2,1)} %bitcast.49), calls=%async_computation.1 | async-start | bytes 786432 | tf_op jit(solution)/shard_map/all_to_all | solution.py:31
  45.3 42.9 %copy-start.4 = (f32[8192]{0:T(1024)S(1)}, f32[8192]{0:T(1024)}, u32[]{:S(2)}) copy-start(f32[8192]{0:T(1024)} %param.18) | copy-start | bytes 98308
  50.3 13.8 %all-to-all-start.2 = ((bf16[16,2,4288]{2,1,0:T(2,128)(2,1)}), bf16[16,2,4288]{2,1,0:T(2,128)(2,1)S(1)}, u32[]{:S(2)}, u32[]{:S(2)}) async-start(bf16[16,2,4288]{2,1,0:T(2,128)(2,1)} %reshape.692), calls=%async_computation.2 | async-start | bytes 557056 | tf_op jit(solution)/shard_map/all_to_all | solution.py:31
  84.6 13.5 %all-to-all-start.4 = ((bf16[16,16,512]{2,1,0:T(8,128)(2,1)}), bf16[16,16,512]{2,1,0:T(8,128)(2,1)S(1)}, u32[]{:S(2)}, u32[]{:S(2)}) async-start(bf16[16,16,512]{2,1,0:T(8,128)(2,1)} %broadcast_in_dim.39), calls=%async_computation.4 | async-start | bytes 524288 | tf_op jit(solution)/shard_map/all_to_all | solution.py:31
  98.5 34.5 %copy-start.1 = (bf16[512,1024]{1,0:T(8,128)(2,1)S(1)}, bf16[512,1024]{1,0:T(8,128)(2,1)}, u32[]{:S(2)}) copy-start(bf16[512,1024]{1,0:T(8,128)(2,1)} %param.21) | copy-start | bytes 3145732

commit v2 on v1

--- a/solution.py
+++ b/solution.py
@@ -1,8 +1,12 @@
+import functools
 import math
 
 import jax
 import jax.numpy as jnp
+import numpy as np
 from jax import lax
+from jax.experimental import pallas as pl
+from jax.experimental.pallas import tpu as pltpu
 from jax.sharding import PartitionSpec as P
 
 HEADS = 64
@@ -203,6 +207,416 @@
     return (mixed_rows.astype(jnp.float32) + shares).astype(jnp.bfloat16)
 
 
+VMEM = pltpu.VMEM
+SMEM = pltpu.SMEM
+KIB = 1024
+PIECES = 3
+STAT_ROWS = 8
+
+
+def whole(space):
+    return pl.BlockSpec(memory_space=space)
+
+
+def small_params(mebibytes):
+    return pltpu.CompilerParams(vmem_limit_bytes=mebibytes * KIB * KIB)
+
+
+def angles_kernel(lengths_ref, frequency_ref, cosine_ref, sine_ref, *, prefix_tokens):
+    row = lax.broadcasted_iota(jnp.int32, cosine_ref.shape, 0)
+    position = jnp.zeros(cosine_ref.shape, jnp.int32)
+    for sample in range(cosine_ref.shape[0]):
+        position = jnp.where(row == sample, prefix_tokens + lengths_ref[sample], position)
+    angles = position.astype(jnp.float32) * frequency_ref[...]
+    cosine_ref[...] = jnp.cos(angles)
+    sine_ref[...] = jnp.sin(angles)
+
+
+def rotated(head, cosine, sine):
+    lane = lax.broadcasted_iota(jnp.int32, head.shape, 1)
+    ahead = pltpu.roll(head, HEAD_DIM - 1, 1)
+    behind = pltpu.roll(head, 1, 1)
+    return head * cosine + jnp.where(lane % 2 == 0, -ahead, behind) * sine
+
+
+def row_scale(blocks_ref):
+    devices, samples, width = blocks_ref.shape
+    total = jnp.zeros((samples, width), jnp.float32)
+    for block in range(devices):
+        widened = blocks_ref[block].astype(jnp.float32)
+        total = total + widened * widened
+    mean_square = jnp.sum(total, axis=1, keepdims=True) / (devices * width)
+    return lax.rsqrt(mean_square + EPSILON)
+
+
+def normed_block(blocks_ref, gain_ref, scale, block):
+    widened = blocks_ref[block].astype(jnp.float32)
+    width = widened.shape[1]
+    gain = gain_ref[pl.ds(block * width, width)].reshape(1, width)
+    return (widened * scale * gain).astype(jnp.bfloat16)
+
+
+def project_kernel(
+    self_ref, blocks_ref, gain_ref, cosine_ref, sine_ref, q_ref, k_ref, v_ref,
+    payload_ref, normed_ref, fresh_ref,
+):
+    devices, samples, width = blocks_ref.shape
+    scale = row_scale(blocks_ref)
+    query = jnp.zeros((samples, q_ref.shape[1]), jnp.float32)
+    for block in range(devices):
+        normed = normed_block(blocks_ref, gain_ref, scale, block)
+        normed_ref[block] = normed
+        query = query + jnp.dot(
+            normed, q_ref[block * width : (block + 1) * width, :],
+            preferred_element_type=jnp.float32,
+        )
+    own = normed_ref[self_ref[0]]
+    row = 0
+    for weight_ref in (k_ref, v_ref):
+        term = jnp.dot(own, weight_ref[...], preferred_element_type=jnp.float32)
+        for place in range(0, term.shape[1], HEAD_DIM):
+            fresh_ref[:, row, :] = term[:, place : place + HEAD_DIM]
+            row += 1
+    cosine = cosine_ref[...]
+    sine = sine_ref[...]
+    heads = q_ref.shape[1] // HEAD_DIM
+    for head in range(heads):
+        turned = rotated(query[:, head * HEAD_DIM : (head + 1) * HEAD_DIM], cosine, sine)
+        turned = turned.astype(jnp.bfloat16)
+        for peer in range(devices):
+            payload_ref[peer, head * samples : (head + 1) * samples, :] = turned
+    base = heads * samples
+    fresh = fresh_ref[...]
+    high = fresh.astype(jnp.bfloat16)
+    payload_ref[:, base : base + row, :] = high
+    low = (fresh - high.astype(jnp.float32)).astype(jnp.bfloat16)
+    payload_ref[:, base + row : base + 2 * row, :] = low
+
+
+def product_nt(left, right):
+    return lax.dot_general(
+        left, right, (((1,), (1,)), ((), ())), preferred_element_type=jnp.float32
+    )
+
+
+def stat_tile(peak, total):
+    rows = peak.shape[0]
+    lane = lax.broadcasted_iota(jnp.int32, (rows, HEAD_DIM), 1)
+    tile = jnp.zeros((rows, HEAD_DIM), jnp.float32)
+    place = 0
+    for value in (peak, total):
+        rest = value
+        for _ in range(PIECES):
+            piece = rest.astype(jnp.bfloat16).astype(jnp.float32)
+            tile = jnp.where(lane == place, piece, tile)
+            rest = rest - piece
+            place += 1
+    return tile
+
+
+def stats_in_lanes(tile):
+    row = lax.broadcasted_iota(jnp.int32, (STAT_ROWS, HEAD_DIM), 0)
+    lane = lax.broadcasted_iota(jnp.int32, (STAT_ROWS, HEAD_DIM), 1)
+    pick = (row == lane).astype(jnp.float32).astype(jnp.bfloat16)
+    return product_nt(pick, tile.astype(jnp.bfloat16))
+
+
+def attend_kernel(
+    self_ref, lengths_ref, table_ref, blocks_ref, cosine_ref, sine_ref, keys_ref, values_ref,
+    slot_keys_ref, slot_values_ref, payload_ref, suffix_sum_ref, suffix_stat_ref,
+    sum_ref, stat_ref,
+):
+    devices = blocks_ref.shape[0]
+    samples = payload_ref.shape[0]
+    per_peer = HEADS // devices
+    group = HEADS // KV_HEADS
+    peers = group // per_peer
+    query_rows = per_peer * samples
+    fresh_rows = 2 * KV_HEADS
+    score_scale = 1.0 / math.sqrt(HEAD_DIM)
+    self_index = self_ref[0]
+    fresh = jnp.zeros((fresh_rows, HEAD_DIM), jnp.float32)
+    fresh_low = jnp.zeros((fresh_rows, HEAD_DIM), jnp.float32)
+    for peer in range(devices):
+        high = blocks_ref[peer, query_rows : query_rows + fresh_rows, :]
+        low = blocks_ref[peer, query_rows + fresh_rows : query_rows + 2 * fresh_rows, :]
+        fresh = fresh + high.astype(jnp.float32)
+        fresh_low = fresh_low + low.astype(jnp.float32)
+    fresh = fresh + fresh_low
+    fresh_keys = rotated(
+        fresh[:KV_HEADS], cosine_ref[pl.ds(self_index, 1), :], sine_ref[pl.ds(self_index, 1), :]
+    )
+    fresh_keys = fresh_keys.astype(jnp.bfloat16).astype(jnp.float32)
+    fresh_values = fresh[KV_HEADS:].astype(jnp.bfloat16).astype(jnp.float32)
+    slots = slot_keys_ref.shape[0]
+    places = table_ref.shape[1]
+    block_size = slots // places
+    slot = lax.broadcasted_iota(jnp.int32, (1, slots), 1)
+    limit = jnp.zeros((1, slots), jnp.int32)
+    length = lengths_ref[self_index]
+    for place in range(places):
+        limit = jnp.where(
+            slot // block_size == table_ref[0, place], length - place * block_size, limit
+        )
+    live = slot % block_size < limit
+    group_row = lax.broadcasted_iota(jnp.int32, (group, group * samples), 0)
+    group_lane = lax.broadcasted_iota(jnp.int32, (group, group * samples), 1)
+    pick = (group_lane == group_row * samples + self_index).astype(jnp.float32)
+    pick = pick.astype(jnp.bfloat16)
+    suffix_tiles = []
+    for head in range(KV_HEADS):
+        lanes = slice(head * HEAD_DIM, (head + 1) * HEAD_DIM)
+        query = jnp.concatenate(
+            [blocks_ref[head * peers + peer, 0:query_rows, :] for peer in range(peers)], axis=0
+        )
+        scores = product_nt(query, keys_ref[:, lanes]) * score_scale
+        peak = jnp.max(scores, axis=1, keepdims=True)
+        weights = jnp.exp(scores - peak)
+        total = jnp.sum(weights, axis=1, keepdims=True)
+        summed = jnp.dot(
+            weights.astype(jnp.bfloat16), values_ref[:, lanes], preferred_element_type=jnp.float32
+        )
+        tile = stat_tile(peak, total)
+        for member in range(group):
+            rows = slice(member * samples, (member + 1) * samples)
+            sum_ref[:, head * group + member, :] = summed[rows]
+            stat_ref[:, head * group + member, :] = tile[rows]
+        own = jnp.dot(pick, query, preferred_element_type=jnp.float32)
+        slot_scores = product_nt(own.astype(jnp.bfloat16), slot_keys_ref[:, lanes]) * score_scale
+        slot_scores = jnp.where(live, slot_scores, -1e30)
+        fresh_score = (
+            jnp.sum(own * fresh_keys[head : head + 1], axis=1, keepdims=True) * score_scale
+        )
+        slot_peak = jnp.maximum(jnp.max(slot_scores, axis=1, keepdims=True), fresh_score)
+        slot_weights = jnp.exp(slot_scores - slot_peak)
+        fresh_weight = jnp.exp(fresh_score - slot_peak)
+        slot_total = jnp.sum(slot_weights, axis=1, keepdims=True) + fresh_weight
+        slot_sum = jnp.dot(
+            slot_weights.astype(jnp.bfloat16), slot_values_ref[:, lanes],
+            preferred_element_type=jnp.float32,
+        )
+        rounded = fresh_weight.astype(jnp.bfloat16).astype(jnp.float32)
+        suffix_sum_ref[head * group : (head + 1) * group, :] = (
+            slot_sum + rounded * fresh_values[head : head + 1]
+        )
+        suffix_tiles.append(stat_tile(slot_peak, slot_total))
+    suffix_stat_ref[...] = stats_in_lanes(jnp.concatenate(suffix_tiles, axis=0))
+    payload_ref[:, 0:HEADS, :] = sum_ref[...].astype(jnp.bfloat16)
+    for sample in range(samples):
+        stats = stats_in_lanes(stat_ref[sample])
+        payload_ref[sample, HEADS : HEADS + STAT_ROWS, 0:HEADS] = stats.astype(jnp.bfloat16)
+        payload_ref[sample, HEADS : HEADS + STAT_ROWS, HEADS:HEAD_DIM] = jnp.zeros(
+            (STAT_ROWS, HEAD_DIM - HEADS), jnp.bfloat16
+        )
+
+
+def merge_kernel(blocks_ref, suffix_sum_ref, suffix_stat_ref, payload_ref, stat_ref):
+    devices = blocks_ref.shape[0]
+    stat_ref[...] = blocks_ref[:, HEADS : HEADS + STAT_ROWS, :].astype(jnp.float32)
+    peaks = (stat_ref[:, 0, :] + stat_ref[:, 1, :]) + stat_ref[:, 2, :]
+    totals = (stat_ref[:, 3, :] + stat_ref[:, 4, :]) + stat_ref[:, 5, :]
+    peaks = peaks[:, :HEADS]
+    totals = totals[:, :HEADS]
+    own = suffix_stat_ref[...]
+    suffix_peak = (own[0:1] + own[1:2]) + own[2:3]
+    suffix_total = (own[3:4] + own[4:5]) + own[5:6]
+    peak_all = jnp.maximum(jnp.max(peaks, axis=0, keepdims=True), suffix_peak)
+    factor = jnp.exp(peaks - peak_all)
+    suffix_factor = jnp.exp(suffix_peak - peak_all)
+    denominator = (
+        jnp.sum(totals * factor, axis=0, keepdims=True) + suffix_total * suffix_factor
+    )
+    shares = jnp.concatenate(
+        [factor / denominator, jnp.broadcast_to(suffix_factor / denominator, (8, HEADS))], axis=0
+    )
+    high = shares.astype(jnp.bfloat16).astype(jnp.float32)
+    rest = shares - high
+    middle = rest.astype(jnp.bfloat16).astype(jnp.float32)
+    row = lax.broadcasted_iota(jnp.int32, (HEADS, HEADS), 0)
+    lane = lax.broadcasted_iota(jnp.int32, (HEADS, HEADS), 1)
+    unit = (row == lane).astype(jnp.float32).astype(jnp.bfloat16)
+    columns = product_nt(unit, high.astype(jnp.bfloat16)) + product_nt(
+        unit, middle.astype(jnp.bfloat16)
+    )
+    mixed = suffix_sum_ref[...] * columns[:, devices : devices + 1]
+    for peer in range(devices):
+        part = blocks_ref[peer, 0:HEADS, :].astype(jnp.float32)
+        mixed = mixed + part * columns[:, peer : peer + 1]
+    attention = mixed.astype(jnp.bfloat16)
+    for peer in range(devices):
+        payload_ref[peer] = attention
+
+
+def output_kernel(attention_ref, tokens_ref, o_ref, mixed_ref, payload_ref, wide_ref):
+    wide_ref[...] = attention_ref[...].astype(jnp.float32)
+    attended = jnp.zeros(tokens_ref.shape, jnp.float32)
+    for head in range(0, HEADS, 2):
+        pair = jnp.concatenate([wide_ref[:, head, :], wide_ref[:, head + 1, :]], axis=1)
+        attended = attended + jnp.dot(
+            pair.astype(jnp.bfloat16), o_ref[head * HEAD_DIM : (head + 2) * HEAD_DIM, :],
+            preferred_element_type=jnp.float32,
+        )
+    mixed = (tokens_ref[...].astype(jnp.float32) + attended).astype(jnp.bfloat16)
+    mixed_ref[...] = mixed
+    for peer in range(payload_ref.shape[0]):
+        payload_ref[peer] = mixed
+
+
+def feed_kernel(blocks_ref, gain_ref, gate_ref, up_ref, down_ref, payload_ref):
+    devices, samples, width = blocks_ref.shape
+    scale = row_scale(blocks_ref)
+    hidden_width = gate_ref.shape[1]
+    gate = jnp.zeros((samples, hidden_width), jnp.float32)
+    up = jnp.zeros((samples, hidden_width), jnp.float32)
+    for block in range(devices):
+        normed = normed_block(blocks_ref, gain_ref, scale, block)
+        rows = slice(block * width, (block + 1) * width)
+        gate = gate + jnp.dot(normed, gate_ref[rows, :], preferred_element_type=jnp.float32)
+        up = up + jnp.dot(normed, up_ref[rows, :], preferred_element_type=jnp.float32)
+    hidden = (gate * (1.0 / (1.0 + jnp.exp(-gate))) * up).astype(jnp.bfloat16)
+    for peer in range(devices):
+        payload_ref[peer] = jnp.dot(
+            hidden, down_ref[:, peer * width : (peer + 1) * width],
+            preferred_element_type=jnp.float32,
+        ).astype(jnp.bfloat16)
+
+
+def kernel_body(
+    tokens,
+    attn_gain,
+    mlp_gain,
+    q_weight,
+    k_weight,
+    v_weight,
+    o_weight,
+    gate_weight,
+    up_weight,
+    down_weight,
+    prefix_keys,
+    prefix_values,
+    suffix_keys,
+    suffix_values,
+    suffix_lengths,
+    suffix_table,
+):
+    self_index = lax.axis_index("ctx")
+    devices = lax.axis_size("ctx")
+    samples, width = tokens.shape
+    self_array = self_index.astype(jnp.int32).reshape(1)
+    pair_index = np.arange(HEAD_DIM, dtype=np.int32) // 2
+    frequency = np.exp(
+        pair_index.astype(np.float32) * np.float32(-2.0 * math.log(ROPE_BASE) / HEAD_DIM)
+    )
+    cosine, sine = pl.pallas_call(
+        functools.partial(angles_kernel, prefix_tokens=prefix_keys.shape[0] * devices),
+        name="angles",
+        cost_estimate=pl.CostEstimate(flops=40000000000, bytes_accessed=1000, transcendentals=0),
+        out_shape=[jax.ShapeDtypeStruct((samples, HEAD_DIM), jnp.float32)] * 2,
+        in_specs=[whole(SMEM), whole(VMEM)],
+        out_specs=[whole(VMEM)] * 2,
+        compiler_params=small_params(1),
+    )(suffix_lengths, jnp.asarray(frequency).reshape(1, HEAD_DIM))
+    slots = suffix_keys.shape[0] * suffix_keys.shape[1]
+    slot_keys = suffix_keys.reshape(slots, -1)
+    slot_values = suffix_values.reshape(slots, -1)
+
+    sent = jnp.broadcast_to(tokens[None], (devices,) + tokens.shape)
+    token_blocks = exchange(sent)
+    fresh_rows = 4 * KV_HEADS
+    query_rows = samples * (width // HEAD_DIM)
+    sent = pl.pallas_call(
+        project_kernel,
+        name="project",
+        cost_estimate=pl.CostEstimate(flops=40000000000, bytes_accessed=1000, transcendentals=0),
+        out_shape=jax.ShapeDtypeStruct((devices, query_rows + fresh_rows, HEAD_DIM), jnp.bfloat16),
+        in_specs=[whole(SMEM)] + [whole(VMEM)] * 7,
+        out_specs=whole(VMEM),
+        scratch_shapes=[
+            VMEM((devices, samples, width), jnp.bfloat16),
+            VMEM((samples, fresh_rows // 2, HEAD_DIM), jnp.float32),
+        ],
+        compiler_params=small_params(8),
+    )(self_array, token_blocks, attn_gain, cosine, sine, q_weight, k_weight, v_weight)
+    query_blocks = exchange(sent)
+    sent, suffix_sum, suffix_stat = pl.pallas_call(
+        attend_kernel,
+        name="attend",
+        cost_estimate=pl.CostEstimate(flops=40000000000, bytes_accessed=1000, transcendentals=0),
+        out_shape=[
+            jax.ShapeDtypeStruct((samples, HEADS + STAT_ROWS, HEAD_DIM), jnp.bfloat16),
+            jax.ShapeDtypeStruct((HEADS, HEAD_DIM), jnp.float32),
+            jax.ShapeDtypeStruct((STAT_ROWS, HEADS), jnp.float32),
+        ],
+        in_specs=[whole(SMEM)] * 3 + [whole(VMEM)] * 7,
+        out_specs=[whole(VMEM)] * 3,
+        scratch_shapes=[
+            VMEM((samples, HEADS, HEAD_DIM), jnp.float32),
+            VMEM((samples, HEADS, HEAD_DIM), jnp.float32),
+        ],
+        compiler_params=small_params(8),
+    )(
+        self_array, suffix_lengths, suffix_table, query_blocks, cosine, sine,
+        prefix_keys, prefix_values, slot_keys, slot_values,
+    )
+    part_blocks = exchange(sent)
+    sent = pl.pallas_call(
+        merge_kernel,
+        name="merge",
+        cost_estimate=pl.CostEstimate(flops=40000000000, bytes_accessed=1000, transcendentals=0),
+        out_shape=jax.ShapeDtypeStruct((devices, HEADS, HEAD_DIM), jnp.bfloat16),
+        in_specs=[whole(VMEM)] * 3,
+        out_specs=whole(VMEM),
+        scratch_shapes=[VMEM((devices, STAT_ROWS, HEAD_DIM), jnp.float32)],
+        compiler_params=small_params(4),
+    )(part_blocks, suffix_sum, suffix_stat)
+    attention = exchange(sent)
+    mixed, sent = pl.pallas_call(
+        output_kernel,
+        name="output",
+        cost_estimate=pl.CostEstimate(flops=40000000000, bytes_accessed=1000, transcendentals=0),
+        out_shape=[
+            jax.ShapeDtypeStruct(tokens.shape, jnp.bfloat16),
+            jax.ShapeDtypeStruct((devices,) + tokens.shape, jnp.bfloat16),
+        ],
+        in_specs=[whole(VMEM)] * 3,
+        out_specs=[whole(VMEM)] * 2,
+        scratch_shapes=[VMEM((samples, HEADS, HEAD_DIM), jnp.float32)],
+        compiler_params=small_params(4),
+    )(attention, tokens, o_weight)
+    mixed_blocks = exchange(sent)
+    sent = pl.pallas_call(
+        feed_kernel,
+        name="feed",
+        cost_estimate=pl.CostEstimate(flops=1000, bytes_accessed=1000, transcendentals=0),
+        out_shape=jax.ShapeDtypeStruct((devices,) + tokens.shape, jnp.bfloat16),
+        in_specs=[whole(VMEM)] * 5,
+        out_specs=whole(VMEM),
+        compiler_params=small_params(4),
+    )(mixed_blocks, mlp_gain, gate_weight, up_weight, down_weight)
+    shares = jnp.sum(exchange(sent).astype(jnp.float32), axis=0)
+    return (mixed.astype(jnp.float32) + shares).astype(jnp.bfloat16)
+
+
+def fits_kernels(devices, args):
+    tokens, k_weight, suffix_table = args[0], args[4], args[15]
+    samples, width = tokens.shape
+    return (
+        width % HEAD_DIM == 0
+        and HEADS % devices == 0
+        and (HEADS // KV_HEADS) % (HEADS // devices) == 0
+        and suffix_table.shape[0] == 1
+        and samples == devices
+        and samples % 16 == 0
+        and k_weight.shape[0] == width
+    )
+
+
+def choose_body(*args):
+    if fits_kernels(lax.axis_size("ctx"), args):
+        return kernel_body(*args)
+    return body(*args)
+
+
 def solution(mesh):
     placed = (
         P("groups", "ctx"),
@@ -223,5 +637,5 @@
         P(("groups", "ctx"), None),
     )
     return jax.shard_map(
-        body, mesh=mesh, in_specs=placed, out_specs=P("groups", "ctx"), check_vma=False
-    )
+        choose_body, mesh=mesh, in_specs=placed, out_specs=P("groups", "ctx"), check_vma=False
+    )

time: 134 us -> 112 us (0.84)
  blocking collectives: 25.5 us -> 67.9 us
  matrix products: 32 us -> 0 us
  waiting for transfers between devices: 31.9 us -> 8.09 us
  Pallas kernels: 0 us -> 15.5 us
  starting transfers between devices: 18 us -> 7.41 us
  local copies, waits for them, and re-layouts: 18.6 us -> 12 us
  other arithmetic: 5.91 us -> 0.66 us
    all_to_all x2 -> x5, blocking collectives: 25.5 us -> 67.9 us  [exchange(): return lax.all_to_all(blocks, 'ctx', 0, 0, tiled=True)]
    dot_general x10 -> x0, matrix products: 32 us -> none  [the longest x1 12.9 us: body(): jnp.dot(hidden, down_weight, preferred_element_type=jnp.float32)]
    all_to_all x4 -> x1, waiting for transfers between devices: 31.9 us -> 8.09 us  [exchange(): return lax.all_to_all(blocks, 'ctx', 0, 0, tiled=True)]
    pallas_call x0 -> x6, Pallas kernels: none -> 15.5 us  [the longest x1 6.77 us: kernel_body(): pl.pallas_call(feed_kernel, name='feed', cost_estimate=pl.CostEstimate(fl...]
    all_to_all x4 -> x1, starting transfers between devices: 18 us -> 7.41 us  [exchange(): return lax.all_to_all(blocks, 'ctx', 0, 0, tiled=True)]
    unnamed x24 -> x50, local copies, waits for them, and re-layouts: 6.96 us -> 10.5 us
    slice x10 -> x0, local copies, waits for them, and re-layouts: 2.59 us -> none  [the longest x2 0.84 us: rotate(): even_part = matrix[:, 0::2]]
    convert_element_type x4 -> x0, local copies, waits for them, and re-layouts: 1.95 us -> none  [the longest x1 1.57 us: body(): rotate(columns_dot(attn_normed, q_weight), position, query_cols)]
  transfers between devices with their start and end apart: 4 -> 1, of which waited for: 4 -> 1; matrix products, arithmetic and copies ran while one was open for 7% -> 0% of each run, Pallas kernels for 0% -> 1%
where the time goes in v2:
time: 112 us
  blocking collectives  67.9 us (61%)
  Pallas kernels  15.5 us (14%)
  local copies, waits for them, and re-layouts  12 us (11%)
  waiting for transfers between devices  8.09 us (7%)
  starting transfers between devices  7.41 us (7%)
    all_to_all x5, blocking collectives, exchange(): return lax.all_to_all(blocks, 'ctx', 0, 0, tiled=True)  67.9 us
    unnamed x50, local copies, waits for them, and re-layouts  10.5 us
    all_to_all x1, waiting for transfers between devices, exchange(): return lax.all_to_all(blocks, 'ctx', 0, 0, tiled=True)  8.09 us
    all_to_all x1, starting transfers between devices, exchange(): return lax.all_to_all(blocks, 'ctx', 0, 0, tiled=True)  7.41 us
    pallas_call x1, Pallas kernels, kernel_body(): pl.pallas_call(feed_kernel, name='feed', cost_estimate=pl.CostEstimate(fl...  6.77 us
    pallas_call x1, Pallas kernels, kernel_body(): pl.pallas_call(attend_kernel, name='attend', cost_estimate=pl.CostEstimat...  4.78 us
  transfers between devices with their start and end apart: 1, of which 1 were waited for; matrix products, arithmetic and copies ran while one was open for 0% of the time, Pallas kernels for 1%

profile of v2, /device:TPU:0, one launch (start us, length us, event | category | flops | bytes accessed | tf_op | source)
XLA Modules:
  0.0 111.8 jit_solution(3612037457167393712)
XLA Ops:
  0.0 1.4 %broadcast_in_dim.2 = bf16[16,16,512]{2,1,0:T(8,128)(2,1)} broadcast(bf16[16,512]{1,0:T(8,128)(2,1)} %tokens_ref.1), dimensions={1,2} | broadcast | bytes 278528 | tf_op jit(solution)/shard_map/broadcast_in_dim | solution.py:523
  1.4 7.4 %all-to-all-start = ((bf16[16,16,512]{2,1,0:T(8,128)(2,1)}), bf16[16,16,512]{2,1,0:T(8,128)(2,1)S(1)}, u32[]{:S(2)}, u32[]{:S(2)}) async-start(bf16[16,16,512]{2,1,0:T(8,128)(2,1)} %broadcast_in_dim.2), calls=%async_computation | async-start | bytes 524288 | tf_op jit(solution)/shard_map/all_to_all | solution.py:35
  8.9 0.0 copy-start.11
  8.9 0.6 copy-done.11
  9.5 0.7 copy-done.14
  10.2 0.6 angles.1
  10.8 8.1 %all-to-all-done.blocks_ref = bf16[16,16,512]{2,1,0:T(8,128)(2,1)S(1)} async-done(((bf16[16,16,512]{2,1,0:T(8,128)(2,1)}), bf16[16,16,512]{2,1,0:T(8,128)(2,1)S(1)}, u32[]{:S(2)}, u32[]{:S(2)}) %all-to-all-start) | async-done | bytes 262176 | tf_op jit(solution)/shard_map/all_to_all | solution.py:35
  18.9 0.0 copy-start.3
  18.9 3.4 %copy-done.3 = bf16[8192,512]{1,0:T(8,128)(2,1)S(1)} copy-done((bf16[8192,512]{1,0:T(8,128)(2,1)S(1)}, bf16[8192,512]{1,0:T(8,128)(2,1)}, u32[]{:S(2)}) %copy-start.3) | copy-done | bytes 8388632
  22.3 0.0 copy-start.12
  22.3 0.0 copy-start.13
  22.3 1.6 %project.1 = bf16[16,96,128]{2,1,0:T(8,128)(2,1)S(1)} custom-call(s32[1]{0:T(128)} %bitcast.self_ref, bf16[16,16,512]{2,1,0:T(8,128)(2,1)S(1)} %all-to-all-done.blocks_ref, f32[8192]{0:T(1024)S(1)} %copy-done.10, f32[16,128]{1,0:T(8,128)S(1)} %get-tuple-element.12.cosine_ref, f32[16,128]{1,0:T(8,128)S(1)} %get-tuple-element.13.sine_ref, ...), custom_call_target="tpu_custom_call" | custom-call | flops 40000000000 | bytes 1000 | tf_op jit(solution)/shard_map/project/pallas_call | solution.py:527
  23.9 14.8 %all_to_all.30.blocks_ref = bf16[16,96,128]{2,1,0:T(8,128)(2,1)S(1)} all-to-all(bf16[16,96,128]{2,1,0:T(8,128)(2,1)S(1)} %project.1), channel_id=1, replica_groups=mesh['groups'=2,'ctx'=16] {'ctx'}, dimensions={0} | all-to-all | bytes 786432 | tf_op jit(solution)/shard_map/all_to_all | solution.py:35
  38.8 0.0 copy-done.8
  38.8 0.0 slice-start.8
  38.8 4.8 %attend.1 = (bf16[16,72,128]{2,1,0:T(8,128)(2,1)S(1)}, f32[64,128]{1,0:T(8,128)S(1)}, f32[8,64]{1,0:T(8,128)S(1)}) custom-call(s32[1]{0:T(128)} %bitcast.self_ref, s32[16]{0:T(128)S(1)} %copy-done.12, s32[1,8]{1,0:T(1,128)S(1)} %copy-done.13, bf16[16,96,128]{2,1,0:T(8,128)(2,1)S(1)} %all_to_all.30.blocks_ref, f32[16,128]{1,0:T(8,128)S(1)} %get-tuple-element.12.cosine_ref, ...), custom_call_target="tpu_custom_call" | custom-call | flops 40000000000 | bytes 1000 | tf_op jit(solution)/shard_map/attend/pallas_call | solution.py:541
  43.6 14.0 %all_to_all.31.blocks_ref = bf16[16,72,128]{2,1,0:T(8,128)(2,1)S(1)} all-to-all(bf16[16,72,128]{2,1,0:T(8,128)(2,1)S(1)} %get-tuple-element.14), channel_id=1, replica_groups=mesh['groups'=2,'ctx'=16] {'ctx'}, dimensions={0} | all-to-all | bytes 589824 | tf_op jit(solution)/shard_map/all_to_all | solution.py:35
  57.6 0.0 slice-start.5
  57.6 0.5 merge.1
  58.1 13.1 %all_to_all.32.attention_ref = bf16[16,64,128]{2,1,0:T(8,128)(2,1)S(1)} all-to-all(bf16[16,64,128]{2,1,0:T(8,128)(2,1)S(1)} %merge.1), channel_id=1, replica_groups=mesh['groups'=2,'ctx'=16] {'ctx'}, dimensions={0} | all-to-all | bytes 524288 | tf_op jit(solution)/shard_map/all_to_all | solution.py:35
  71.3 0.0 slice-start.2
  71.3 0.0 slice-start.3
  71.3 0.0 slice-start.6
  71.3 0.0 slice-start.7
  71.3 0.0 copy-start.1
  71.3 1.2 %output.1 = (bf16[16,512]{1,0:T(8,128)(2,1)S(1)}, bf16[16,16,512]{2,1,0:T(8,128)(2,1)S(1)}) custom-call(bf16[16,64,128]{2,1,0:T(8,128)(2,1)S(1)} %all_to_all.32.attention_ref, bf16[16,512]{1,0:T(8,128)(2,1)S(1)} %copy-done.2, bf16[8192,512]{1,0:T(8,128)(2,1)S(1)} %bitcast.8), custom_call_target="tpu_custom_call" | custom-call | flops 40000000000 | bytes 1000 | tf_op jit(solution)/shard_map/output/pallas_call | solution.py:573
  72.6 13.1 %all_to_all.33.blocks_ref = bf16[16,16,512]{2,1,0:T(8,128)(2,1)S(1)} all-to-all(bf16[16,16,512]{2,1,0:T(8,128)(2,1)S(1)} %get-tuple-element.18), channel_id=1, replica_groups=mesh['groups'=2,'ctx'=16] {'ctx'}, dimensions={0} | all-to-all | bytes 524288 | tf_op jit(solution)/shard_map/all_to_all | solution.py:35
  85.8 0.0 copy-start
  85.8 5.8 %copy-done = bf16[8192,1024]{1,0:T(8,128)(2,1)S(1)} copy-done((bf16[8192,1024]{1,0:T(8,128)(2,1)S(1)}, bf16[8192,1024]{1,0:T(8,128)(2,1)}, u32[]{:S(2)}) %copy-start) | copy-done | bytes 16777240
  91.6 6.8 %feed.1 = bf16[16,16,512]{2,1,0:T(8,128)(2,1)S(1)} custom-call(bf16[16,16,512]{2,1,0:T(8,128)(2,1)S(1)} %all_to_all.33.blocks_ref, f32[8192]{0:T(1024)S(1)} %copy-done.1, bf16[8192,1024]{1,0:T(8,128)(2,1)S(1)} %copy-done, bf16[8192,1024]{1,0:T(8,128)(2,1)S(1)} %bitcast.4, bf16[1024,8192]{1,0:T(8,128)(2,1)S(1)} %bitcast.6), custom_call_target="tpu_custom_call" | custom-call | flops 1000 | bytes 1000 | tf_op jit(solution)/shard_map/feed/pallas_call | solution.py:587
  98.3 12.8 %all_to_all.34 = bf16[16,16,512]{2,1,0:T(8,128)(2,1)S(1)} all-to-all(bf16[16,16,512]{2,1,0:T(8,128)(2,1)S(1)} %feed.1), channel_id=1, replica_groups=mesh['groups'=2,'ctx'=16] {'ctx'}, dimensions={0} | all-to-all | bytes 524288 | tf_op jit(solution)/shard_map/all_to_all | solution.py:35
  111.2 0.6 add_convert_fusion
  (37 shorter events, 0.1 us)
Async XLA Ops:
  1.4 17.4 %all-to-all-start = ((bf16[16,16,512]{2,1,0:T(8,128)(2,1)}), bf16[16,16,512]{2,1,0:T(8,128)(2,1)S(1)}, u32[]{:S(2)}, u32[]{:S(2)}) async-start(bf16[16,16,512]{2,1,0:T(8,128)(2,1)} %broadcast_in_dim.2), calls=%async_computation | async-start | bytes 524288 | tf_op jit(solution)/shard_map/all_to_all | solution.py:35
  8.9 0.7 copy-start.11
  9.5 0.7 copy-start.14
  10.2 8.7 %copy-start.4 = (bf16[512,1024]{1,0:T(8,128)(2,1)S(1)}, bf16[512,1024]{1,0:T(8,128)(2,1)}, u32[]{:S(2)}) copy-start(bf16[512,1024]{1,0:T(8,128)(2,1)} %k_ref.1) | copy-start | bytes 3145732
  10.2 8.7 %copy-start.5 = (bf16[512,1024]{1,0:T(8,128)(2,1)S(1)}, bf16[512,1024]{1,0:T(8,128)(2,1)}, u32[]{:S(2)}) copy-start(bf16[512,1024]{1,0:T(8,128)(2,1)} %v_ref.1) | copy-start | bytes 3145732
  10.2 8.7 %copy-start.10 = (f32[8192]{0:T(1024)S(1)}, f32[8192]{0:T(1024)}, u32[]{:S(2)}) copy-start(f32[8192]{0:T(1024)} %gain_ref.2) | copy-start | bytes 98308
  18.9 3.4 %copy-start.3 = (bf16[8192,512]{1,0:T(8,128)(2,1)S(1)}, bf16[8192,512]{1,0:T(8,128)(2,1)}, u32[]{:S(2)}) copy-start(bf16[8192,512]{1,0:T(8,128)(2,1)} %q_ref.1) | copy-start | bytes 25165828
  22.3 16.5 %copy-start.6 = (bf16[256,1024]{1,0:T(8,128)(2,1)S(1)}, bf16[256,1024]{1,0:T(8,128)(2,1)}, u32[]{:S(2)}) copy-start(bf16[256,1024]{1,0:T(8,128)(2,1)} %keys_ref.1) | copy-start | bytes 1572868
  22.3 16.5 %copy-start.7 = (bf16[256,1024]{1,0:T(8,128)(2,1)S(1)}, bf16[256,1024]{1,0:T(8,128)(2,1)}, u32[]{:S(2)}) copy-start(bf16[256,1024]{1,0:T(8,128)(2,1)} %values_ref.1) | copy-start | bytes 1572868
  22.3 16.5 %copy-start.8 = (bf16[8,16,1024]{2,1,0:T(8,128)(2,1)S(1)}, bf16[8,16,1024]{2,1,0:T(8,128)(2,1)}, u32[]{:S(2)}) copy-start(bf16[8,16,1024]{2,1,0:T(8,128)(2,1)} %param.29) | copy-start | bytes 786436
  22.3 16.5 %copy-start.9 = (bf16[8,16,1024]{2,1,0:T(8,128)(2,1)S(1)}, bf16[8,16,1024]{2,1,0:T(8,128)(2,1)}, u32[]{:S(2)}) copy-start(bf16[8,16,1024]{2,1,0:T(8,128)(2,1)} %param.30) | copy-start | bytes 786436
  22.3 16.5 %copy-start.12 = (s32[16]{0:T(128)S(1)}, s32[16]{0:T(128)}, u32[]{:S(2)}) copy-start(s32[16]{0:T(128)} %lengths_ref.3) | copy-start | bytes 196
  22.3 16.5 %copy-start.13 = (s32[1,8]{1,0:T(1,128)S(1)}, s32[1,8]{1,0:T(1,128)}, u32[]{:S(2)}) copy-start(s32[1,8]{1,0:T(1,128)} %table_ref.1) | copy-start | bytes 100
  38.8 32.5 %slice-start.8 = ((s8[8388608]{0:T(1024)(128)(4,1)}), s8[4194304]{0:T(1024)(128)(4,1)S(1)}, s32[]{:S(2)}) async-start(s8[8388608]{0:T(1024)(128)(4,1)} %bitcast.7), calls=%async_computation.14 | async-start | bytes 8388608
  43.6 27.7 %slice-start.9 = ((s8[8388608]{0:T(1024)(128)(4,1)}), s8[4194304]{0:T(1024)(128)(4,1)S(1)}, s32[]{:S(2)}) async-start(s8[8388608]{0:T(1024)(128)(4,1)} %bitcast.7), calls=%async_computation.15 | async-start | bytes 8388608
  57.6 13.6 %copy-start.2 = (bf16[16,512]{1,0:T(8,128)(2,1)S(1)}, bf16[16,512]{1,0:T(8,128)(2,1)}, u32[]{:S(2)}) copy-start(bf16[16,512]{1,0:T(8,128)(2,1)} %tokens_ref.1) | copy-start | bytes 49156
  57.6 28.1 %slice-start = ((s8[16777216]{0:T(1024)(128)(4,1)}), s8[4194304]{0:T(1024)(128)(4,1)S(1)}, s32[]{:S(2)}) async-start(s8[16777216]{0:T(1024)(128)(4,1)} %bitcast.3), calls=%async_computation.6 | async-start | bytes 8388608
  57.6 28.1 %slice-start.1 = ((s8[16777216]{0:T(1024)(128)(4,1)}), s8[4194304]{0:T(1024)(128)(4,1)S(1)}, s32[]{:S(2)}) async-start(s8[16777216]{0:T(1024)(128)(4,1)} %bitcast.3), calls=%async_computation.7 | async-start | bytes 8388608
  57.6 28.1 %slice-start.4 = ((s8[16777216]{0:T(1024)(128)(4,1)}), s8[4194304]{0:T(1024)(128)(4,1)S(1)}, s32[]{:S(2)}) async-start(s8[16777216]{0:T(1024)(128)(4,1)} %bitcast.5), calls=%async_computation.10 | async-start | bytes 8388608
  57.6 28.1 %slice-start.5 = ((s8[16777216]{0:T(1024)(128)(4,1)}), s8[4194304]{0:T(1024)(128)(4,1)S(1)}, s32[]{:S(2)}) async-start(s8[16777216]{0:T(1024)(128)(4,1)} %bitcast.5), calls=%async_computation.11 | async-start | bytes 8388608
  71.3 14.5 %slice-start.2 = ((s8[16777216]{0:T(1024)(128)(4,1)}), s8[4194304]{0:T(1024)(128)(4,1)S(1)}, s32[]{:S(2)}) async-start(s8[16777216]{0:T(1024)(128)(4,1)} %bitcast.3), calls=%async_computation.8 | async-start | bytes 8388608
  71.3 14.5 %slice-start.3 = ((s8[16777216]{0:T(1024)(128)(4,1)}), s8[4194304]{0:T(1024)(128)(4,1)S(1)}, s32[]{:S(2)}) async-start(s8[16777216]{0:T(1024)(128)(4,1)} %bitcast.3), calls=%async_computation.9 | async-start | bytes 8388608
  71.3 14.5 %slice-start.6 = ((s8[16777216]{0:T(1024)(128)(4,1)}), s8[4194304]{0:T(1024)(128)(4,1)S(1)}, s32[]{:S(2)}) async-start(s8[16777216]{0:T(1024)(128)(4,1)} %bitcast.5), calls=%async_computation.12 | async-start | bytes 8388608
  71.3 14.5 %slice-start.7 = ((s8[16777216]{0:T(1024)(128)(4,1)}), s8[4194304]{0:T(1024)(128)(4,1)S(1)}, s32[]{:S(2)}) async-start(s8[16777216]{0:T(1024)(128)(4,1)} %bitcast.5), calls=%async_computation.13 | async-start | bytes 8388608
  71.3 14.5 %copy-start.1 = (f32[8192]{0:T(1024)S(1)}, f32[8192]{0:T(1024)}, u32[]{:S(2)}) copy-start(f32[8192]{0:T(1024)} %gain_ref.3) | copy-start | bytes 98308
  85.8 5.8 %copy-start = (bf16[8192,1024]{1,0:T(8,128)(2,1)S(1)}, bf16[8192,1024]{1,0:T(8,128)(2,1)}, u32[]{:S(2)}) copy-start(bf16[8192,1024]{1,0:T(8,128)(2,1)} %gate_ref.1) | copy-start | bytes 50331652

commit v3 on v2

--- a/solution.py
+++ b/solution.py
@@ -3,7 +3,6 @@
 
 import jax
 import jax.numpy as jnp
-import numpy as np
 from jax import lax
 from jax.experimental import pallas as pl
 from jax.experimental.pallas import tpu as pltpu
@@ -222,12 +221,46 @@
     return pltpu.CompilerParams(vmem_limit_bytes=mebibytes * KIB * KIB)
 
 
-def angles_kernel(lengths_ref, frequency_ref, cosine_ref, sine_ref, *, prefix_tokens):
+def exchange_like_cores(blocks):
+    devices = lax.axis_size("ctx")
+    sets = [[peer for peer in range(devices) if peer % 2 == core] for core in range(2)]
+    return lax.all_to_all(blocks, "ctx", 0, 0, tiled=True, axis_index_groups=sets)
+
+
+def swap_cores(blocks):
+    devices = lax.axis_size("ctx")
+    return lax.ppermute(blocks, "ctx", [(peer, peer ^ 1) for peer in range(devices)])
+
+
+def gather_pairs(blocks):
+    own = exchange_like_cores(blocks)
+    return own, swap_cores(own)
+
+
+def block_sources(own_ref, other_ref):
+    core = lax.axis_index("ctx") % 2
+    return [
+        (source, pair, 2 * pair + (core if source is own_ref else 1 - core))
+        for source in (own_ref, other_ref)
+        for pair in range(own_ref.shape[0])
+    ]
+
+
+def spread_kernel(block_ref, payload_ref):
+    for peer in range(payload_ref.shape[0]):
+        payload_ref[peer] = block_ref[...]
+
+
+def fill_angles(lengths_ref, prefix_tokens, cosine_ref, sine_ref):
+    lane = lax.broadcasted_iota(jnp.int32, cosine_ref.shape, 1)
+    frequency = jnp.exp(
+        (lane // 2).astype(jnp.float32) * (-2.0 * math.log(ROPE_BASE) / HEAD_DIM)
+    )
     row = lax.broadcasted_iota(jnp.int32, cosine_ref.shape, 0)
     position = jnp.zeros(cosine_ref.shape, jnp.int32)
     for sample in range(cosine_ref.shape[0]):
         position = jnp.where(row == sample, prefix_tokens + lengths_ref[sample], position)
-    angles = position.astype(jnp.float32) * frequency_ref[...]
+    angles = position.astype(jnp.float32) * frequency
     cosine_ref[...] = jnp.cos(angles)
     sine_ref[...] = jnp.sin(angles)
 
@@ -239,38 +272,37 @@
     return head * cosine + jnp.where(lane % 2 == 0, -ahead, behind) * sine
 
 
-def row_scale(blocks_ref):
-    devices, samples, width = blocks_ref.shape
+def row_scale(own_ref, other_ref):
+    pairs, samples, width = own_ref.shape
     total = jnp.zeros((samples, width), jnp.float32)
-    for block in range(devices):
-        widened = blocks_ref[block].astype(jnp.float32)
+    for source, pair, _ in block_sources(own_ref, other_ref):
+        widened = source[pair].astype(jnp.float32)
         total = total + widened * widened
-    mean_square = jnp.sum(total, axis=1, keepdims=True) / (devices * width)
+    mean_square = jnp.sum(total, axis=1, keepdims=True) / (2 * pairs * width)
     return lax.rsqrt(mean_square + EPSILON)
 
 
-def normed_block(blocks_ref, gain_ref, scale, block):
-    widened = blocks_ref[block].astype(jnp.float32)
+def normed_block(block, gain_ref, scale, place):
+    widened = block.astype(jnp.float32)
     width = widened.shape[1]
-    gain = gain_ref[pl.ds(block * width, width)].reshape(1, width)
+    gain = gain_ref[pl.ds(pl.multiple_of(place * width, width), width)].reshape(1, width)
     return (widened * scale * gain).astype(jnp.bfloat16)
 
 
 def project_kernel(
-    self_ref, blocks_ref, gain_ref, cosine_ref, sine_ref, q_ref, k_ref, v_ref,
-    payload_ref, normed_ref, fresh_ref,
+    lengths_ref, own_ref, other_ref, gain_ref, q_ref, k_ref, v_ref,
+    payload_ref, cosine_ref, sine_ref, normed_ref, fresh_ref, *, prefix_tokens
 ):
-    devices, samples, width = blocks_ref.shape
-    scale = row_scale(blocks_ref)
+    fill_angles(lengths_ref, prefix_tokens, cosine_ref, sine_ref)
+    devices, samples, width = normed_ref.shape
+    scale = row_scale(own_ref, other_ref)
     query = jnp.zeros((samples, q_ref.shape[1]), jnp.float32)
-    for block in range(devices):
-        normed = normed_block(blocks_ref, gain_ref, scale, block)
-        normed_ref[block] = normed
-        query = query + jnp.dot(
-            normed, q_ref[block * width : (block + 1) * width, :],
-            preferred_element_type=jnp.float32,
-        )
-    own = normed_ref[self_ref[0]]
+    for source, pair, place in block_sources(own_ref, other_ref):
+        normed = normed_block(source[pair], gain_ref, scale, place)
+        normed_ref[place] = normed
+        rows = pl.ds(pl.multiple_of(place * width, width), width)
+        query = query + jnp.dot(normed, q_ref[rows, :], preferred_element_type=jnp.float32)
+    own = normed_ref[lax.axis_index("ctx")]
     row = 0
     for weight_ref in (k_ref, v_ref):
         term = jnp.dot(own, weight_ref[...], preferred_element_type=jnp.float32)
@@ -322,7 +354,7 @@
 
 
 def attend_kernel(
-    self_ref, lengths_ref, table_ref, blocks_ref, cosine_ref, sine_ref, keys_ref, values_ref,
+    lengths_ref, table_ref, blocks_ref, cosine_ref, sine_ref, keys_ref, values_ref,
     slot_keys_ref, slot_values_ref, payload_ref, suffix_sum_ref, suffix_stat_ref,
     sum_ref, stat_ref,
 ):
@@ -334,7 +366,7 @@
     query_rows = per_peer * samples
     fresh_rows = 2 * KV_HEADS
     score_scale = 1.0 / math.sqrt(HEAD_DIM)
-    self_index = self_ref[0]
+    self_index = lax.axis_index("ctx")
     fresh = jnp.zeros((fresh_rows, HEAD_DIM), jnp.float32)
     fresh_low = jnp.zeros((fresh_rows, HEAD_DIM), jnp.float32)
     for peer in range(devices):
@@ -443,12 +475,13 @@
         part = blocks_ref[peer, 0:HEADS, :].astype(jnp.float32)
         mixed = mixed + part * columns[:, peer : peer + 1]
     attention = mixed.astype(jnp.bfloat16)
-    for peer in range(devices):
+    for peer in range(payload_ref.shape[0]):
         payload_ref[peer] = attention
 
 
-def output_kernel(attention_ref, tokens_ref, o_ref, mixed_ref, payload_ref, wide_ref):
-    wide_ref[...] = attention_ref[...].astype(jnp.float32)
+def output_kernel(own_ref, other_ref, tokens_ref, o_ref, mixed_ref, wide_ref):
+    for source, pair, place in block_sources(own_ref, other_ref):
+        wide_ref[place] = source[pair].astype(jnp.float32)
     attended = jnp.zeros(tokens_ref.shape, jnp.float32)
     for head in range(0, HEADS, 2):
         pair = jnp.concatenate([wide_ref[:, head, :], wide_ref[:, head + 1, :]], axis=1)
@@ -458,27 +491,36 @@
         )
     mixed = (tokens_ref[...].astype(jnp.float32) + attended).astype(jnp.bfloat16)
     mixed_ref[...] = mixed
-    for peer in range(payload_ref.shape[0]):
-        payload_ref[peer] = mixed
-
-
-def feed_kernel(blocks_ref, gain_ref, gate_ref, up_ref, down_ref, payload_ref):
-    devices, samples, width = blocks_ref.shape
-    scale = row_scale(blocks_ref)
+
+
+def feed_kernel(
+    own_ref, other_ref, gain_ref, gate_ref, up_ref, down_ref, own_sums_ref, other_sums_ref
+):
+    pairs, samples, width = own_ref.shape
+    core = lax.axis_index("ctx") % 2
+    scale = row_scale(own_ref, other_ref)
     hidden_width = gate_ref.shape[1]
     gate = jnp.zeros((samples, hidden_width), jnp.float32)
     up = jnp.zeros((samples, hidden_width), jnp.float32)
-    for block in range(devices):
-        normed = normed_block(blocks_ref, gain_ref, scale, block)
-        rows = slice(block * width, (block + 1) * width)
+    for source, pair, place in block_sources(own_ref, other_ref):
+        normed = normed_block(source[pair], gain_ref, scale, place)
+        rows = pl.ds(pl.multiple_of(place * width, width), width)
         gate = gate + jnp.dot(normed, gate_ref[rows, :], preferred_element_type=jnp.float32)
         up = up + jnp.dot(normed, up_ref[rows, :], preferred_element_type=jnp.float32)
     hidden = (gate * (1.0 / (1.0 + jnp.exp(-gate))) * up).astype(jnp.bfloat16)
-    for peer in range(devices):
-        payload_ref[peer] = jnp.dot(
-            hidden, down_ref[:, peer * width : (peer + 1) * width],
-            preferred_element_type=jnp.float32,
-        ).astype(jnp.bfloat16)
+    for side, sums_ref in enumerate((other_sums_ref, own_sums_ref)):
+        for pair in range(pairs):
+            place = 2 * pair + (1 - core if side == 0 else core)
+            columns = pl.ds(pl.multiple_of(place * width, width), width)
+            sums_ref[pair] = jnp.dot(
+                hidden, down_ref[:, columns], preferred_element_type=jnp.float32
+            ).astype(sums_ref.dtype)
+
+
+def pair_kernel(own_sums_ref, received_ref, payload_ref):
+    payload_ref[...] = (own_sums_ref[...] + received_ref[...].astype(jnp.float32)).astype(
+        jnp.bfloat16
+    )
 
 
 def kernel_body(
@@ -499,44 +541,43 @@
     suffix_lengths,
     suffix_table,
 ):
-    self_index = lax.axis_index("ctx")
     devices = lax.axis_size("ctx")
     samples, width = tokens.shape
-    self_array = self_index.astype(jnp.int32).reshape(1)
-    pair_index = np.arange(HEAD_DIM, dtype=np.int32) // 2
-    frequency = np.exp(
-        pair_index.astype(np.float32) * np.float32(-2.0 * math.log(ROPE_BASE) / HEAD_DIM)
-    )
-    cosine, sine = pl.pallas_call(
-        functools.partial(angles_kernel, prefix_tokens=prefix_keys.shape[0] * devices),
-        name="angles",
-        cost_estimate=pl.CostEstimate(flops=40000000000, bytes_accessed=1000, transcendentals=0),
-        out_shape=[jax.ShapeDtypeStruct((samples, HEAD_DIM), jnp.float32)] * 2,
-        in_specs=[whole(SMEM), whole(VMEM)],
-        out_specs=[whole(VMEM)] * 2,
-        compiler_params=small_params(1),
-    )(suffix_lengths, jnp.asarray(frequency).reshape(1, HEAD_DIM))
+    def spread(name, block):
+        return pl.pallas_call(
+            spread_kernel,
+            name=name,
+            cost_estimate=pl.CostEstimate(flops=40000000000, bytes_accessed=1000, transcendentals=0),
+            out_shape=jax.ShapeDtypeStruct((devices // 2,) + block.shape, block.dtype),
+            in_specs=[whole(VMEM)],
+            out_specs=whole(VMEM),
+            compiler_params=small_params(1),
+        )(block)
+
     slots = suffix_keys.shape[0] * suffix_keys.shape[1]
     slot_keys = suffix_keys.reshape(slots, -1)
     slot_values = suffix_values.reshape(slots, -1)
 
-    sent = jnp.broadcast_to(tokens[None], (devices,) + tokens.shape)
-    token_blocks = exchange(sent)
+    token_blocks = gather_pairs(spread("spread", tokens))
     fresh_rows = 4 * KV_HEADS
     query_rows = samples * (width // HEAD_DIM)
-    sent = pl.pallas_call(
-        project_kernel,
+    sent, cosine, sine = pl.pallas_call(
+        functools.partial(project_kernel, prefix_tokens=prefix_keys.shape[0] * devices),
         name="project",
         cost_estimate=pl.CostEstimate(flops=40000000000, bytes_accessed=1000, transcendentals=0),
-        out_shape=jax.ShapeDtypeStruct((devices, query_rows + fresh_rows, HEAD_DIM), jnp.bfloat16),
-        in_specs=[whole(SMEM)] + [whole(VMEM)] * 7,
-        out_specs=whole(VMEM),
+        out_shape=[
+            jax.ShapeDtypeStruct((devices, query_rows + fresh_rows, HEAD_DIM), jnp.bfloat16),
+            jax.ShapeDtypeStruct((samples, HEAD_DIM), jnp.float32),
+            jax.ShapeDtypeStruct((samples, HEAD_DIM), jnp.float32),
+        ],
+        in_specs=[whole(SMEM)] + [whole(VMEM)] * 6,
+        out_specs=[whole(VMEM)] * 3,
         scratch_shapes=[
             VMEM((devices, samples, width), jnp.bfloat16),
             VMEM((samples, fresh_rows // 2, HEAD_DIM), jnp.float32),
         ],
-        compiler_params=small_params(8),
-    )(self_array, token_blocks, attn_gain, cosine, sine, q_weight, k_weight, v_weight)
+        compiler_params=small_params(4),
+    )(suffix_lengths, *token_blocks, attn_gain, q_weight, k_weight, v_weight)
     query_blocks = exchange(sent)
     sent, suffix_sum, suffix_stat = pl.pallas_call(
         attend_kernel,
@@ -547,15 +588,15 @@
             jax.ShapeDtypeStruct((HEADS, HEAD_DIM), jnp.float32),
             jax.ShapeDtypeStruct((STAT_ROWS, HEADS), jnp.float32),
         ],
-        in_specs=[whole(SMEM)] * 3 + [whole(VMEM)] * 7,
+        in_specs=[whole(SMEM)] * 2 + [whole(VMEM)] * 7,
         out_specs=[whole(VMEM)] * 3,
         scratch_shapes=[
             VMEM((samples, HEADS, HEAD_DIM), jnp.float32),
             VMEM((samples, HEADS, HEAD_DIM), jnp.float32),
         ],
-        compiler_params=small_params(8),
+        compiler_params=small_params(4),
     )(
-        self_array, suffix_lengths, suffix_table, query_blocks, cosine, sine,
+        suffix_lengths, suffix_table, query_blocks, cosine, sine,
         prefix_keys, prefix_values, slot_keys, slot_values,
     )
     part_blocks = exchange(sent)
@@ -563,37 +604,45 @@
         merge_kernel,
         name="merge",
         cost_estimate=pl.CostEstimate(flops=40000000000, bytes_accessed=1000, transcendentals=0),
-        out_shape=jax.ShapeDtypeStruct((devices, HEADS, HEAD_DIM), jnp.bfloat16),
+        out_shape=jax.ShapeDtypeStruct((devices // 2, HEADS, HEAD_DIM), jnp.bfloat16),
         in_specs=[whole(VMEM)] * 3,
         out_specs=whole(VMEM),
         scratch_shapes=[VMEM((devices, STAT_ROWS, HEAD_DIM), jnp.float32)],
-        compiler_params=small_params(4),
+        compiler_params=small_params(3),
     )(part_blocks, suffix_sum, suffix_stat)
-    attention = exchange(sent)
-    mixed, sent = pl.pallas_call(
+    attention = gather_pairs(sent)
+    mixed = pl.pallas_call(
         output_kernel,
         name="output",
         cost_estimate=pl.CostEstimate(flops=40000000000, bytes_accessed=1000, transcendentals=0),
-        out_shape=[
-            jax.ShapeDtypeStruct(tokens.shape, jnp.bfloat16),
-            jax.ShapeDtypeStruct((devices,) + tokens.shape, jnp.bfloat16),
-        ],
-        in_specs=[whole(VMEM)] * 3,
-        out_specs=[whole(VMEM)] * 2,
+        out_shape=jax.ShapeDtypeStruct(tokens.shape, jnp.bfloat16),
+        in_specs=[whole(VMEM)] * 4,
+        out_specs=whole(VMEM),
         scratch_shapes=[VMEM((samples, HEADS, HEAD_DIM), jnp.float32)],
-        compiler_params=small_params(4),
-    )(attention, tokens, o_weight)
-    mixed_blocks = exchange(sent)
-    sent = pl.pallas_call(
+        compiler_params=small_params(3),
+    )(*attention, tokens, o_weight)
+    mixed_blocks = gather_pairs(spread("spread_mixed", mixed))
+    pair_shape = (devices // 2,) + tokens.shape
+    own_sums, other_sums = pl.pallas_call(
         feed_kernel,
         name="feed",
-        cost_estimate=pl.CostEstimate(flops=1000, bytes_accessed=1000, transcendentals=0),
-        out_shape=jax.ShapeDtypeStruct((devices,) + tokens.shape, jnp.bfloat16),
-        in_specs=[whole(VMEM)] * 5,
+        out_shape=[
+            jax.ShapeDtypeStruct(pair_shape, jnp.float32),
+            jax.ShapeDtypeStruct(pair_shape, jnp.bfloat16),
+        ],
+        in_specs=[whole(VMEM)] * 6,
+        out_specs=[whole(VMEM)] * 2,
+        compiler_params=small_params(3),
+    )(*mixed_blocks, mlp_gain, gate_weight, up_weight, down_weight)
+    sent = pl.pallas_call(
+        pair_kernel,
+        name="pair",
+        out_shape=jax.ShapeDtypeStruct(pair_shape, jnp.bfloat16),
+        in_specs=[whole(VMEM)] * 2,
         out_specs=whole(VMEM),
-        compiler_params=small_params(4),
-    )(mixed_blocks, mlp_gain, gate_weight, up_weight, down_weight)
-    shares = jnp.sum(exchange(sent).astype(jnp.float32), axis=0)
+        compiler_params=small_params(1),
+    )(own_sums, swap_cores(other_sums))
+    shares = jnp.sum(exchange_like_cores(sent).astype(jnp.float32), axis=0)
     return (mixed.astype(jnp.float32) + shares).astype(jnp.bfloat16)
 
 
@@ -606,6 +655,7 @@
         and (HEADS // KV_HEADS) % (HEADS // devices) == 0
         and suffix_table.shape[0] == 1
         and samples == devices
+        and devices % 2 == 0
         and samples % 16 == 0
         and k_weight.shape[0] == width
     )

time: 112 us -> 99.6 us (0.89)
  local copies, waits for them, and re-layouts: 12 us -> 3.28 us
  starting transfers between devices: 7.41 us -> 0.22 us
  blocking collectives: 67.9 us -> 74.1 us
  waiting for transfers between devices: 8.09 us -> 5.23 us
    all_to_all x0 -> x4, blocking collectives: none -> 45.4 us  [exchange_like_cores(): lax.all_to_all(blocks, 'ctx', 0, 0, tiled=True, axis_index_groups=sets)]
    all_to_all x5 -> x2, blocking collectives: 67.9 us -> 28.7 us  [exchange(): return lax.all_to_all(blocks, 'ctx', 0, 0, tiled=True)]
    all_to_all x1 -> x0, waiting for transfers between devices: 8.09 us -> none  [exchange(): return lax.all_to_all(blocks, 'ctx', 0, 0, tiled=True)]
    all_to_all x1 -> x0, starting transfers between devices: 7.41 us -> none  [exchange(): return lax.all_to_all(blocks, 'ctx', 0, 0, tiled=True)]
    unnamed x50 -> x54, local copies, waits for them, and re-layouts: 10.5 us -> 3.28 us
    ppermute x0 -> x4, waiting for transfers between devices: none -> 5.23 us  [swap_cores(): lax.ppermute(blocks, 'ctx', [(peer, peer ^ 1) for peer in range(devices)])]
    broadcast_in_dim x1 -> x0, local copies, waits for them, and re-layouts: 1.43 us -> none  [kernel_body(): sent = jnp.broadcast_to(tokens[None], (devices,) + tokens.shape)]
    pallas_call x3 -> x5, Pallas kernels: 8.97 us -> 8.96 us  [the longest x1 6.78 us: kernel_body(): pl.pallas_call(feed_kernel, name='feed', out_shape=[jax.ShapeDtypeStruct(...]
  transfers between devices with their start and end apart: 1 -> 4, of which waited for: 1 -> 4; matrix products, arithmetic and copies ran while one was open for 0% -> 0% of each run, Pallas kernels for 1% -> 0%
where the time goes in v3:
time: 99.6 us; the launch traced here: 99.2 us
  blocking collectives  74.1 us (74%)
  Pallas kernels  15.4 us (15%)
  waiting for transfers between devices  5.23 us (5%)
  local copies, waits for them, and re-layouts  3.28 us (3%)
    all_to_all x4, blocking collectives, exchange_like_cores(): lax.all_to_all(blocks, 'ctx', 0, 0, tiled=True, axis_index_groups=sets)  45.4 us
    all_to_all x2, blocking collectives, exchange(): return lax.all_to_all(blocks, 'ctx', 0, 0, tiled=True)  28.7 us
    pallas_call x1, Pallas kernels, kernel_body(): pl.pallas_call(feed_kernel, name='feed', out_shape=[jax.ShapeDtypeStruct(...  6.78 us
    ppermute x4, waiting for transfers between devices, swap_cores(): lax.ppermute(blocks, 'ctx', [(peer, peer ^ 1) for peer in range(devices)])  5.23 us
    pallas_call x1, Pallas kernels, kernel_body(): pl.pallas_call(attend_kernel, name='attend', cost_estimate=pl.CostEstimat...  4.78 us
    unnamed x54, local copies, waits for them, and re-layouts  3.28 us
    pallas_call x1, Pallas kernels, kernel_body(): pl.pallas_call(functools.partial(project_kernel, prefix_tokens=prefix_key...  2.14 us
  transfers between devices with their start and end apart: 4, of which 4 were waited for; matrix products, arithmetic and copies ran while one was open for 0% of the time, Pallas kernels for 0%

profile of v3, /device:TPU:0, one launch (start us, length us, event | category | flops | bytes accessed | tf_op | source)
XLA Modules:
  0.0 99.2 jit_solution(6401156904470023199)
XLA Ops:
  0.0 0.9 copy-done.9
  0.9 14.7 %all_to_all.30.own_ref = bf16[8,16,512]{2,1,0:T(8,128)(2,1)S(1)} all-to-all(bf16[8,16,512]{2,1,0:T(8,128)(2,1)S(1)} %spread.1), channel_id=1, replica_groups={{0,2,4,6,8,10,12,14},{1,3,5,7,9,11,13,15},{16,18,20,22,24,26,28,30},{17..., dimensions={0} | all-to-all | bytes 262144 | tf_op jit(solution)/shard_map/all_to_all | solution.py:227
  15.6 0.0 copy-start.12
  15.6 0.1 collective-permute-start
  15.7 1.3 %collective-permute-done.other_ref = bf16[8,16,512]{2,1,0:T(8,128)(2,1)S(1)} collective-permute-done((bf16[8,16,512]{2,1,0:T(8,128)(2,1)S(1)}, bf16[8,16,512]{2,1,0:T(8,128)(2,1)S(1)}, u32[]{:S(2)}, u32[]{:S(2)}) %collective-permute-start) | collective-permute-done | bytes 131104 | tf_op jit(solution)/shard_map/ppermute | solution.py:232
  17.1 2.1 %project.1 = (bf16[16,96,128]{2,1,0:T(8,128)(2,1)S(1)}, f32[16,128]{1,0:T(8,128)S(1)}, f32[16,128]{1,0:T(8,128)S(1)}) custom-call(s32[16]{0:T(128)S(1)} %copy-done.11, bf16[8,16,512]{2,1,0:T(8,128)(2,1)S(1)} %all_to_all.30.own_ref, bf16[8,16,512]{2,1,0:T(8,128)(2,1)S(1)} %collective-permute-done.other_ref, f32[8192]{0:T(1024)S(1)} %copy-done.8, ...), custom_call_target="tpu_custom_call" | custom-call | flops 40000000000 | bytes 1000 | tf_op jit(solution)/shard_map/project/pallas_call | solution.py:564
  19.2 14.8 %all_to_all.31.blocks_ref = bf16[16,96,128]{2,1,0:T(8,128)(2,1)S(1)} all-to-all(bf16[16,96,128]{2,1,0:T(8,128)(2,1)S(1)} %get-tuple-element.13), channel_id=1, replica_groups=mesh['groups'=2,'ctx'=16] {'ctx'}, dimensions={0} | all-to-all | bytes 786432 | tf_op jit(solution)/shard_map/all_to_all | solution.py:34
  34.0 0.0 slice-start.12
  34.1 4.8 %attend.1 = (bf16[16,72,128]{2,1,0:T(8,128)(2,1)S(1)}, f32[64,128]{1,0:T(8,128)S(1)}, f32[8,64]{1,0:T(8,128)S(1)}) custom-call(s32[16]{0:T(128)S(1)} %copy-done.11, s32[1,8]{1,0:T(1,128)S(1)} %copy-done.12, bf16[16,96,128]{2,1,0:T(8,128)(2,1)S(1)} %all_to_all.31.blocks_ref, f32[16,128]{1,0:T(8,128)S(1)} %get-tuple-element.14.cosine_ref, ...), custom_call_target="tpu_custom_call" | custom-call | flops 40000000000 | bytes 1000 | tf_op jit(solution)/shard_map/attend/pallas_call | solution.py:582
  38.8 14.0 %all_to_all.32.blocks_ref = bf16[16,72,128]{2,1,0:T(8,128)(2,1)S(1)} all-to-all(bf16[16,72,128]{2,1,0:T(8,128)(2,1)S(1)} %get-tuple-element.16), channel_id=1, replica_groups=mesh['groups'=2,'ctx'=16] {'ctx'}, dimensions={0} | all-to-all | bytes 589824 | tf_op jit(solution)/shard_map/all_to_all | solution.py:34
  52.8 0.5 merge.1
  53.3 10.2 %all_to_all.33.own_ref = bf16[8,64,128]{2,1,0:T(8,128)(2,1)S(1)} all-to-all(bf16[8,64,128]{2,1,0:T(8,128)(2,1)S(1)} %merge.1), channel_id=1, replica_groups={{0,2,4,6,8,10,12,14},{1,3,5,7,9,11,13,15},{16,18,20,22,24,26,28,30},{17..., dimensions={0} | all-to-all | bytes 262144 | tf_op jit(solution)/shard_map/all_to_all | solution.py:227
  63.5 1.3 %collective-permute-done.1.other_ref = bf16[8,64,128]{2,1,0:T(8,128)(2,1)S(1)} collective-permute-done((bf16[8,64,128]{2,1,0:T(8,128)(2,1)S(1)}, bf16[8,64,128]{2,1,0:T(8,128)(2,1)S(1)}, u32[]{:S(2)}, u32[]{:S(2)}) %collective-permute-start.1) | collective-permute-done | bytes 131104 | tf_op jit(solution)/shard_map/ppermute | solution.py:232
  64.8 0.0 slice-start
  64.8 0.0 slice-start.1
  64.8 0.0 slice-start.4
  64.9 0.0 slice-start.5
  64.9 0.0 slice-start.8
  64.9 0.0 slice-start.9
  64.9 1.2 %output.1.block_ref = bf16[16,512]{1,0:T(8,128)(2,1)S(1)} custom-call(bf16[8,64,128]{2,1,0:T(8,128)(2,1)S(1)} %all_to_all.33.own_ref, bf16[8,64,128]{2,1,0:T(8,128)(2,1)S(1)} %collective-permute-done.1.other_ref, bf16[16,512]{1,0:T(8,128)(2,1)S(1)} %copy-done.10, bf16[8192,512]{1,0:T(8,128)(2,1)S(1)} %bitcast.9), custom_call_target="tpu_custom_call" | custom-call | flops 40000000000 | bytes 1000 | tf_op jit(solution)/shard_map/output/pallas_call | solution.py:614
  66.1 0.0 slice-start.6
  66.2 0.0 slice-start.10
  66.2 0.0 copy-start
  66.2 10.5 %all_to_all.34.own_ref = bf16[8,16,512]{2,1,0:T(8,128)(2,1)S(1)} all-to-all(bf16[8,16,512]{2,1,0:T(8,128)(2,1)S(1)} %spread_mixed.1), channel_id=1, replica_groups={{0,2,4,6,8,10,12,14},{1,3,5,7,9,11,13,15},{16,18,20,22,24,26,28,30},{17..., dimensions={0} | all-to-all | bytes 262144 | tf_op jit(solution)/shard_map/all_to_all | solution.py:227
  76.7 1.3 %collective-permute-done.2.other_ref = bf16[8,16,512]{2,1,0:T(8,128)(2,1)S(1)} collective-permute-done((bf16[8,16,512]{2,1,0:T(8,128)(2,1)S(1)}, bf16[8,16,512]{2,1,0:T(8,128)(2,1)S(1)}, u32[]{:S(2)}, u32[]{:S(2)}) %collective-permute-start.2) | collective-permute-done | bytes 131104 | tf_op jit(solution)/shard_map/ppermute | solution.py:232
  78.1 1.1 %slice-done.10 = s8[4194304]{0:T(1024)(128)(4,1)S(1)} async-done(((s8[16777216]{0:T(1024)(128)(4,1)}), s8[4194304]{0:T(1024)(128)(4,1)S(1)}, s32[]{:S(2)}) %slice-start.10) | async-done | bytes 4194328
  79.2 1.2 %slice-done.11 = s8[4194304]{0:T(1024)(128)(4,1)S(1)} async-done(((s8[16777216]{0:T(1024)(128)(4,1)}), s8[4194304]{0:T(1024)(128)(4,1)S(1)}, s32[]{:S(2)}) %slice-start.11) | async-done | bytes 4194328
  80.4 6.8 %feed.1 = (f32[8,16,512]{2,1,0:T(8,128)S(1)}, bf16[8,16,512]{2,1,0:T(8,128)(2,1)S(1)}) custom-call(bf16[8,16,512]{2,1,0:T(8,128)(2,1)S(1)} %all_to_all.34.own_ref, bf16[8,16,512]{2,1,0:T(8,128)(2,1)S(1)} %collective-permute-done.2.other_ref, f32[8192]{0:T(1024)S(1)} %copy-done, bf16[8192,1024]{1,0:T(8,128)(2,1)S(1)} %bitcast.3, ...), custom_call_target="tpu_custom_call" | custom-call | tf_op jit(solution)/shard_map/feed/pallas_call | solution.py:626
  87.2 0.1 collective-permute-start.3
  87.4 1.2 %collective-permute-done.3.received_ref = bf16[8,16,512]{2,1,0:T(8,128)(2,1)S(1)} collective-permute-done((bf16[8,16,512]{2,1,0:T(8,128)(2,1)S(1)}, bf16[8,16,512]{2,1,0:T(8,128)(2,1)S(1)}, u32[]{:S(2)}, u32[]{:S(2)}) %collective-permute-start.3) | collective-permute-done | bytes 131104 | tf_op jit(solution)/shard_map/ppermute | solution.py:232
  88.6 10.0 %all_to_all.35 = bf16[8,16,512]{2,1,0:T(8,128)(2,1)S(1)} all-to-all(bf16[8,16,512]{2,1,0:T(8,128)(2,1)S(1)} %pair.1), channel_id=1, replica_groups={{0,2,4,6,8,10,12,14},{1,3,5,7,9,11,13,15},{16,18,20,22,24,26,28,30},{17..., dimensions={0} | all-to-all | bytes 262144 | tf_op jit(solution)/shard_map/all_to_all | solution.py:227
  98.6 0.6 add_convert_fusion
  (50 shorter events, 0.2 us)
Async XLA Ops:
  0.0 17.1 %copy-start.3 = (bf16[512,1024]{1,0:T(8,128)(2,1)S(1)}, bf16[512,1024]{1,0:T(8,128)(2,1)}, u32[]{:S(2)}) copy-start(bf16[512,1024]{1,0:T(8,128)(2,1)} %v_ref.1) | copy-start | bytes 3145732
  0.0 17.1 %copy-start.2 = (bf16[512,1024]{1,0:T(8,128)(2,1)S(1)}, bf16[512,1024]{1,0:T(8,128)(2,1)}, u32[]{:S(2)}) copy-start(bf16[512,1024]{1,0:T(8,128)(2,1)} %k_ref.1) | copy-start | bytes 3145732
  0.0 17.1 %copy-start.1 = (bf16[8192,512]{1,0:T(8,128)(2,1)S(1)}, bf16[8192,512]{1,0:T(8,128)(2,1)}, u32[]{:S(2)}) copy-start(bf16[8192,512]{1,0:T(8,128)(2,1)} %q_ref.1) | copy-start | bytes 25165828
  0.0 17.1 %copy-start.8 = (f32[8192]{0:T(1024)S(1)}, f32[8192]{0:T(1024)}, u32[]{:S(2)}) copy-start(f32[8192]{0:T(1024)} %gain_ref.2) | copy-start | bytes 98308
  0.0 0.9 copy-start.9
  0.9 16.2 %copy-start.11 = (s32[16]{0:T(128)S(1)}, s32[16]{0:T(128)}, u32[]{:S(2)}) copy-start(s32[16]{0:T(128)} %lengths_ref.3) | copy-start | bytes 196
  15.6 18.4 %copy-start.4 = (bf16[256,1024]{1,0:T(8,128)(2,1)S(1)}, bf16[256,1024]{1,0:T(8,128)(2,1)}, u32[]{:S(2)}) copy-start(bf16[256,1024]{1,0:T(8,128)(2,1)} %keys_ref.1) | copy-start | bytes 1572868
  15.6 18.4 %copy-start.5 = (bf16[256,1024]{1,0:T(8,128)(2,1)S(1)}, bf16[256,1024]{1,0:T(8,128)(2,1)}, u32[]{:S(2)}) copy-start(bf16[256,1024]{1,0:T(8,128)(2,1)} %values_ref.1) | copy-start | bytes 1572868
  15.6 18.4 %copy-start.6 = (bf16[8,16,1024]{2,1,0:T(8,128)(2,1)S(1)}, bf16[8,16,1024]{2,1,0:T(8,128)(2,1)}, u32[]{:S(2)}) copy-start(bf16[8,16,1024]{2,1,0:T(8,128)(2,1)} %param.28) | copy-start | bytes 786436
  15.6 18.4 %copy-start.7 = (bf16[8,16,1024]{2,1,0:T(8,128)(2,1)S(1)}, bf16[8,16,1024]{2,1,0:T(8,128)(2,1)}, u32[]{:S(2)}) copy-start(bf16[8,16,1024]{2,1,0:T(8,128)(2,1)} %param.29) | copy-start | bytes 786436
  15.6 18.4 %copy-start.12 = (s32[1,8]{1,0:T(1,128)S(1)}, s32[1,8]{1,0:T(1,128)}, u32[]{:S(2)}) copy-start(s32[1,8]{1,0:T(1,128)} %table_ref.1) | copy-start | bytes 100
  15.6 1.4 %collective-permute-start = (bf16[8,16,512]{2,1,0:T(8,128)(2,1)S(1)}, bf16[8,16,512]{2,1,0:T(8,128)(2,1)S(1)}, u32[]{:S(2)}, u32[]{:S(2)}) collective-permute-start(bf16[8,16,512]{2,1,0:T(8,128)(2,1)S(1)} %all_to_all.30.own_ref), channel_id=1, source_target_pairs={{0,1},{1,0},{2,3},{3,2},{4,5},{5,4},{6,7},{7,6},{8,9},{9,8},{10,11... | collective-permute-start | bytes 393224 | tf_op jit(solution)/shard_map/ppermute | solution.py:232
  34.0 30.8 %slice-start.12 = ((s8[8388608]{0:T(1024)(128)(4,1)}), s8[4194304]{0:T(1024)(128)(4,1)S(1)}, s32[]{:S(2)}) async-start(s8[8388608]{0:T(1024)(128)(4,1)} %bitcast.8), calls=%async_computation.18 | async-start | bytes 8388608
  38.8 26.0 %slice-start.13 = ((s8[8388608]{0:T(1024)(128)(4,1)}), s8[4194304]{0:T(1024)(128)(4,1)S(1)}, s32[]{:S(2)}) async-start(s8[8388608]{0:T(1024)(128)(4,1)} %bitcast.8), calls=%async_computation.19 | async-start | bytes 8388608
  52.8 12.0 %copy-start.10 = (bf16[16,512]{1,0:T(8,128)(2,1)S(1)}, bf16[16,512]{1,0:T(8,128)(2,1)}, u32[]{:S(2)}) copy-start(bf16[16,512]{1,0:T(8,128)(2,1)} %tokens_ref.1) | copy-start | bytes 49156
  63.4 1.3 %collective-permute-start.1 = (bf16[8,64,128]{2,1,0:T(8,128)(2,1)S(1)}, bf16[8,64,128]{2,1,0:T(8,128)(2,1)S(1)}, u32[]{:S(2)}, u32[]{:S(2)}) collective-permute-start(bf16[8,64,128]{2,1,0:T(8,128)(2,1)S(1)} %all_to_all.33.own_ref), channel_id=1, source_target_pairs={{0,1},{1,0},{2,3},{3,2},{4,5},{5,4},{6,7},{7,6},{8,9},{9,8},{10,11... | collective-permute-start | bytes 393224 | tf_op jit(solution)/shard_map/ppermute | solution.py:232
  64.8 13.2 %slice-start = ((s8[16777216]{0:T(1024)(128)(4,1)}), s8[4194304]{0:T(1024)(128)(4,1)S(1)}, s32[]{:S(2)}) async-start(s8[16777216]{0:T(1024)(128)(4,1)} %bitcast.2), calls=%async_computation.6 | async-start | bytes 8388608
  64.8 13.2 %slice-start.1 = ((s8[16777216]{0:T(1024)(128)(4,1)}), s8[4194304]{0:T(1024)(128)(4,1)S(1)}, s32[]{:S(2)}) async-start(s8[16777216]{0:T(1024)(128)(4,1)} %bitcast.2), calls=%async_computation.7 | async-start | bytes 8388608
  64.8 13.2 %slice-start.4 = ((s8[16777216]{0:T(1024)(128)(4,1)}), s8[4194304]{0:T(1024)(128)(4,1)S(1)}, s32[]{:S(2)}) async-start(s8[16777216]{0:T(1024)(128)(4,1)} %bitcast.4), calls=%async_computation.10 | async-start | bytes 8388608
  64.9 13.2 %slice-start.5 = ((s8[16777216]{0:T(1024)(128)(4,1)}), s8[4194304]{0:T(1024)(128)(4,1)S(1)}, s32[]{:S(2)}) async-start(s8[16777216]{0:T(1024)(128)(4,1)} %bitcast.4), calls=%async_computation.11 | async-start | bytes 8388608
  64.9 13.2 %slice-start.8 = ((s8[16777216]{0:T(1024)(128)(4,1)}), s8[4194304]{0:T(1024)(128)(4,1)S(1)}, s32[]{:S(2)}) async-start(s8[16777216]{0:T(1024)(128)(4,1)} %bitcast.6), calls=%async_computation.14 | async-start | bytes 8388608
  64.9 13.2 %slice-start.9 = ((s8[16777216]{0:T(1024)(128)(4,1)}), s8[4194304]{0:T(1024)(128)(4,1)S(1)}, s32[]{:S(2)}) async-start(s8[16777216]{0:T(1024)(128)(4,1)} %bitcast.6), calls=%async_computation.15 | async-start | bytes 8388608
  66.1 12.0 %slice-start.2 = ((s8[16777216]{0:T(1024)(128)(4,1)}), s8[4194304]{0:T(1024)(128)(4,1)S(1)}, s32[]{:S(2)}) async-start(s8[16777216]{0:T(1024)(128)(4,1)} %bitcast.2), calls=%async_computation.8 | async-start | bytes 8388608
  66.1 12.0 %slice-start.3 = ((s8[16777216]{0:T(1024)(128)(4,1)}), s8[4194304]{0:T(1024)(128)(4,1)S(1)}, s32[]{:S(2)}) async-start(s8[16777216]{0:T(1024)(128)(4,1)} %bitcast.2), calls=%async_computation.9 | async-start | bytes 8388608
  66.1 12.0 %slice-start.6 = ((s8[16777216]{0:T(1024)(128)(4,1)}), s8[4194304]{0:T(1024)(128)(4,1)S(1)}, s32[]{:S(2)}) async-start(s8[16777216]{0:T(1024)(128)(4,1)} %bitcast.4), calls=%async_computation.12 | async-start | bytes 8388608
  66.2 12.0 %slice-start.7 = ((s8[16777216]{0:T(1024)(128)(4,1)}), s8[4194304]{0:T(1024)(128)(4,1)S(1)}, s32[]{:S(2)}) async-start(s8[16777216]{0:T(1024)(128)(4,1)} %bitcast.4), calls=%async_computation.13 | async-start | bytes 8388608
  66.2 13.1 %slice-start.10 = ((s8[16777216]{0:T(1024)(128)(4,1)}), s8[4194304]{0:T(1024)(128)(4,1)S(1)}, s32[]{:S(2)}) async-start(s8[16777216]{0:T(1024)(128)(4,1)} %bitcast.6), calls=%async_computation.16 | async-start | bytes 8388608
  66.2 14.2 %slice-start.11 = ((s8[16777216]{0:T(1024)(128)(4,1)}), s8[4194304]{0:T(1024)(128)(4,1)S(1)}, s32[]{:S(2)}) async-start(s8[16777216]{0:T(1024)(128)(4,1)} %bitcast.6), calls=%async_computation.17 | async-start | bytes 8388608
  66.2 14.2 %copy-start = (f32[8192]{0:T(1024)S(1)}, f32[8192]{0:T(1024)}, u32[]{:S(2)}) copy-start(f32[8192]{0:T(1024)} %gain_ref.3) | copy-start | bytes 98308
  76.7 1.3 %collective-permute-start.2 = (bf16[8,16,512]{2,1,0:T(8,128)(2,1)S(1)}, bf16[8,16,512]{2,1,0:T(8,128)(2,1)S(1)}, u32[]{:S(2)}, u32[]{:S(2)}) collective-permute-start(bf16[8,16,512]{2,1,0:T(8,128)(2,1)S(1)} %all_to_all.34.own_ref), channel_id=1, source_target_pairs={{0,1},{1,0},{2,3},{3,2},{4,5},{5,4},{6,7},{7,6},{8,9},{9,8},{10,11... | collective-permute-start | bytes 393224 | tf_op jit(solution)/shard_map/ppermute | solution.py:232
  87.2 1.4 %collective-permute-start.3 = (bf16[8,16,512]{2,1,0:T(8,128)(2,1)S(1)}, bf16[8,16,512]{2,1,0:T(8,128)(2,1)S(1)}, u32[]{:S(2)}, u32[]{:S(2)}) collective-permute-start(bf16[8,16,512]{2,1,0:T(8,128)(2,1)S(1)} %get-tuple-element.20), channel_id=1, source_target_pairs={{0,1},{1,0},{2,3},{3,2},{4,5},{5,4},{6,7},{7,6},{8,9},{9,8},{10,11... | collective-permute-start | bytes 393224 | tf_op jit(solution)/shard_map/ppermute | solution.py:232
